TPU v7x, 32 devices: a whole 2x2x4 slice. The times are simulated.
32 devices in a mesh: groups: 2 (over x), ctx: 8 (over z, y), tp: 2 (over core).
Axes of the slice: x: 2, y: 2, z: 4, core: 2. Of those that a mesh axis runs over, the one named last changes fastest.
Arguments:
- enc_input: bfloat16 [2048, 4096], P(('groups', 'ctx')), parts along dimension 0, may hold values from -6 to 6
- enc_query: bfloat16 [2048, 1024], P(('groups', 'ctx'), 'tp'), parts along dimension 0
- enc_key: bfloat16 [2048, 1024], P(('groups', 'ctx'), 'tp'), parts along dimension 0
- enc_value: bfloat16 [2048, 1024], P(('groups', 'ctx'), 'tp'), parts along dimension 0, may hold values from -6 to 6
- seq_length: int32 [2], P('groups'), parts along dimension 0, may hold values from 256 to 1024
- attn_out_weight: bfloat16 [1024, 4096], P('tp'), may hold values from -0.1875 to 0.1875
- enc_gain: bfloat16 [4096], replicated, may hold values from 0.25 to 1.75
- cross_key_weight: bfloat16 [4096, 1024], P('ctx', 'tp'), may hold values from -0.09375 to 0.09375
- cross_value_weight: bfloat16 [4096, 1024], P('ctx', 'tp'), may hold values from -0.09375 to 0.09375
- embed_table: bfloat16 [32128, 4096], P('tp', 'ctx')
- dec_ids: int32 [32, 2], P('groups'), parts along dimension 0, may hold values from 0 to 32127
- dec_gain: bfloat16 [4096], P('ctx'), may hold values from 0.25 to 1.75
- cross_query_weight: bfloat16 [4096, 1024], P('ctx', 'tp')
- cross_out_weight: bfloat16 [1024, 4096], P('tp', 'ctx'), may hold values from -0.1875 to 0.1875
Outputs:
- cross_keys: bfloat16 [16, 128, 1024], P(('groups', 'ctx'), None, 'tp'), parts along dimension 0
- cross_values: bfloat16 [16, 128, 1024], P(('groups', 'ctx'), None, 'tp'), parts along dimension 0
- decoded: bfloat16 [32, 2, 4096], P('groups', None, 'ctx'), parts along dimension 0
There are 2 independent parts, one for each index of `groups`. A program takes and returns all parts, laid end to end along the dimension named above; an argument that names none is the same for every part. Nothing has to cross between parts.
Inputs may be any that keep to these rules, and one draw needn't show every extreme that they name: `seq_length`: the input's real length.
All inputs are finite; a program needn't handle non-finite values.
Results may differ from a plain program's by a relative error of at most 0.04.
Values may be sent and summed in bfloat16 or wider, within the bound.
A program may use at most 128 MiB of HBM per device.

v0:
```python
import math

import jax
import jax.numpy as jnp
from jax import lax
from jax.experimental import pallas as pl
from jax.experimental.pallas import tpu as pltpu
from jax.sharding import PartitionSpec as P

D = 4096
HD = 128


EPSILON = 1e-06
FLOOR = -1e30


def joined(value, axis, join):
    pieces = jax.tree.map(lambda part: lax.all_gather(part, axis), value)
    head = jax.tree.map(lambda part: part[0], pieces)
    tail = jax.tree.map(lambda part: part[1:], pieces)
    total, _ = lax.scan(lambda total, piece: (join(total, piece), None), head, tail)
    return total


def softmax_merge(first, second):
    top_first, total_first, mixed_first = first
    top_second, total_second, mixed_second = second
    top = jnp.maximum(top_first, top_second)
    weight_first = jnp.exp(top_first - top)
    weight_second = jnp.exp(top_second - top)
    total = total_first * weight_first + total_second * weight_second
    mixed = mixed_first * weight_first[..., None] + mixed_second * weight_second[..., None]
    return (top, total, mixed)


def partial_softmax(queries, keys, values, valid, factor):
    scores = jnp.einsum("qhd,khd->hqk", queries, keys, preferred_element_type=jnp.float32) * factor
    scores = jnp.where(valid[None, None, :], scores, FLOOR)
    top = jnp.max(scores, axis=-1)
    probs = jnp.where(valid[None, None, :], jnp.exp(scores - top[..., None]), 0.0)
    total = jnp.sum(probs, axis=-1)
    mixed = jnp.einsum(
        "hqk,khd->hqd", probs.astype(jnp.bfloat16), values, preferred_element_type=jnp.float32
    )
    return (top, total, mixed)


def norm_rows(resid, gain):
    scale = lax.rsqrt(jnp.mean(resid * resid, axis=-1, keepdims=True) + EPSILON)
    return (resid * scale * gain.astype(jnp.float32)).astype(jnp.bfloat16)


def local(
    enc_input,
    enc_query,
    enc_key,
    enc_value,
    seq_length,
    attn_out_weight,
    enc_gain,
    cross_key_weight,
    cross_value_weight,
    embed_table,
    dec_ids,
    dec_gain,
    cross_query_weight,
    cross_out_weight,
):
    rows, inner_local = enc_query.shape
    heads_local = inner_local // HD
    limit = seq_length[0]
    queries = enc_query.reshape(rows, heads_local, HD)
    start_state = (
        jnp.full((heads_local, rows), FLOOR, jnp.float32),
        jnp.zeros((heads_local, rows), jnp.float32),
        jnp.zeros((heads_local, rows, HD), jnp.float32),
    )
    carry = start_state
    key_rows = lax.all_gather(enc_key, "ctx", axis=0, tiled=True)
    value_rows = lax.all_gather(enc_value, "ctx", axis=0, tiled=True)
    count = key_rows.shape[0]
    block = math.gcd(count, 2048)
    blocks = count // block
    key_blocks = key_rows.reshape(blocks, block, heads_local, HD)
    value_blocks = value_rows.reshape(blocks, block, heads_local, HD)
    offsets = jnp.arange(blocks, dtype=jnp.int32) * block

    def one_block(state, item):
        key_block, value_block, offset = item
        positions = offset + jnp.arange(block, dtype=jnp.int32)
        update = partial_softmax(queries, key_block, value_block, positions < limit, HD ** (-0.5))
        return (softmax_merge(state, update), None)

    carry, unused = lax.scan(one_block, carry, (key_blocks, value_blocks, offsets))
    top, total, mixed = carry
    context = (
        jnp.transpose(mixed / total[..., None], (1, 0, 2))
        .reshape(rows, inner_local)
        .astype(jnp.bfloat16)
    )
    summed = lax.psum(jnp.dot(context, attn_out_weight, preferred_element_type=jnp.float32), "tp")
    memory = norm_rows(enc_input.astype(jnp.float32) + summed, enc_gain)
    ctx_count = lax.axis_size("ctx")
    slots = rows // ctx_count
    key_sum = jnp.dot(
        memory,
        lax.all_gather(cross_key_weight, "ctx", axis=0, tiled=True),
        preferred_element_type=jnp.float32,
    )
    value_sum = jnp.dot(
        memory,
        lax.all_gather(cross_value_weight, "ctx", axis=0, tiled=True),
        preferred_element_type=jnp.float32,
    )
    key_rows = key_sum.astype(jnp.bfloat16)
    value_rows = value_sum.astype(jnp.bfloat16)
    keys_moved, values_moved = (
        lax.all_to_all(
            key_rows.reshape(slots, ctx_count, inner_local),
            "ctx",
            split_axis=1,
            concat_axis=0,
            tiled=True,
        ),
        lax.all_to_all(
            value_rows.reshape(slots, ctx_count, inner_local),
            "ctx",
            split_axis=1,
            concat_axis=0,
            tiled=True,
        ),
    )
    keys_cache = keys_moved.reshape(rows, inner_local)
    values_cache = values_moved.reshape(rows, inner_local)
    beams = dec_ids.shape[0]
    vocab_local = embed_table.shape[0]
    flat_ids = dec_ids.reshape(-1) - lax.axis_index("tp") * vocab_local
    inside = (flat_ids >= 0) & (flat_ids < vocab_local)
    looked = jnp.take(embed_table, jnp.clip(flat_ids, 0, vocab_local - 1), axis=0)
    own_rows = jnp.where(inside[:, None], looked.astype(jnp.float32), 0.0)
    hidden = lax.psum(own_rows.astype(jnp.bfloat16), "tp").astype(jnp.float32)
    scaled = (hidden * dec_gain.astype(jnp.float32)).astype(jnp.bfloat16)
    raw_part = jnp.dot(scaled, cross_query_weight, preferred_element_type=jnp.float32)
    square_part = jnp.sum(hidden * hidden, axis=-1)
    raw, squares = lax.psum((raw_part, square_part), "ctx")
    factor = lax.rsqrt(squares / D + EPSILON)
    query = (raw * factor[:, None] * HD ** (-0.5)).astype(jnp.bfloat16).reshape(-1, heads_local, HD)
    positions = jnp.arange(rows, dtype=jnp.int32) * ctx_count + lax.axis_index("ctx")
    local_part = partial_softmax(
        query,
        keys_cache.reshape(rows, heads_local, HD),
        values_cache.reshape(rows, heads_local, HD),
        positions < limit,
        1.0,
    )
    top_all, total_all, mixed_all = joined(local_part, "ctx", softmax_merge)
    attn = (
        jnp.transpose(mixed_all / total_all[..., None], (1, 0, 2))
        .reshape(-1, inner_local)
        .astype(jnp.bfloat16)
    )
    out_part = jnp.dot(attn, cross_out_weight, preferred_element_type=jnp.float32)
    out = lax.psum(out_part, "tp")
    decoded = (out + hidden).astype(jnp.bfloat16).reshape(beams, 2, -1)
    return (keys_cache[None], values_cache[None], decoded)


MESH = pl.DeviceIdType.MESH
F32 = jnp.float32
BF16 = jnp.bfloat16
SUBS = 4
CHUNKS = 2


def pick_kernel(ids_ref, length_ref, table_ref, out_ref, enc_mask, dec_mask, held, rows, sems):
    count = out_ref.shape[0]
    vocab_local = table_ref.shape[0]
    base = lax.axis_index("tp") * vocab_local
    copies = []
    for j in range(count):
        own = jnp.clip(ids_ref[j] - base, 0, vocab_local - 1)
        start = pl.multiple_of(lax.div(own, 16) * 16, 16)
        copy = pltpu.make_async_copy(table_ref.at[pl.ds(start, 16)], held.at[j], sems.at[j])
        copy.start()
        copies.append(copy)
    limit = length_ref[0]
    enc_mask[...] = (lax.broadcasted_iota(jnp.int32, enc_mask.shape, 1) < limit).astype(F32)
    places = lax.broadcasted_iota(jnp.int32, dec_mask.shape, 1) * 8 + lax.axis_index("ctx")
    dec_mask[...] = (places < limit).astype(F32)
    spots = lax.broadcasted_iota(jnp.int32, held.shape[1:], 0)
    for j in range(count):
        copies[j].wait()
        own = ids_ref[j] - base
        inside = (own >= 0) & (own < vocab_local)
        spot = jnp.where(inside, lax.rem(jnp.clip(own, 0, vocab_local - 1), 16), -1)
        block = held[j].astype(F32)
        rows[pl.ds(j, 1)] = jnp.sum(jnp.where(spots == spot, block, 0.0), axis=0, keepdims=True)
    out_ref[...] = rows[...].astype(BF16)


def hand_kernel(keys_ref, values_ref, decoded_ref, keys_out, values_out, decoded_out):
    keys_out[0] = keys_ref[...]
    values_out[0] = values_ref[...]
    for i in range(decoded_out.shape[0]):
        decoded_out[i] = decoded_ref[2 * i : 2 * i + 2].astype(BF16)


def fused_kernel(
    q, k, v, ein, looked, dec_gain, wq, wo, enc_gain, wk_far, wv_far, wout_far, valid_enc, valid_dec,
    keys_out, values_out, decoded_out,
    looked_far, wo_all, qg, kg, vg, ein_all, ctx_all, raw_own, raw_out, raw_in, query_in, query_all,
    wk, wv, wout, gained_all, part_k, part_v, slot_k, slot_v, square_out, square_in,
    mixed_out, mixed_in, stats_out, stats_in, proj_out, proj_in, hidden_ref,
    send, r_look, r_wo, r_q, r_k, r_v, r_raw, r_query, r_ein, r_ein_far, r_ctx, r_square, r_ring, r_mixed,
    r_stats, r_proj, fetched,
):
    c = lax.axis_index("ctx")
    t = lax.axis_index("tp")
    z, y = lax.div(c, 2), lax.rem(c, 2)
    mate, other = c + 1 - 2 * y, 1 - t
    line = [lax.rem(z + d, 4) for d in range(1, 4)]
    peers = [lax.rem(c + d, 8) for d in range(1, 8)]
    rows = q.shape[0]
    width = wq.shape[0]
    pending = []

    def put(source, target, arrival, to_ctx, to_tp):
        copy = pltpu.make_async_remote_copy(
            src_ref=source, dst_ref=target, send_sem=send, recv_sem=arrival,
            device_id={"ctx": to_ctx, "tp": to_tp}, device_id_type=MESH,
        )
        copy.start()
        pending.append(copy)

    def got(target, arrival):
        pltpu.make_async_remote_copy(
            src_ref=target, dst_ref=target, send_sem=send, recv_sem=arrival,
            device_id={"ctx": mate, "tp": t}, device_id_type=MESH,
        ).wait_recv()

    def fetch(source, target, arrival):
        copy = pltpu.make_async_copy(source, target, arrival)
        copy.start()
        return copy

    def cols(index, size):
        return pl.ds(pl.multiple_of(index * size, size), size)

    barrier = pltpu.get_barrier_semaphore()
    for peer in peers:
        pl.semaphore_signal(barrier, inc=1, device_id={"ctx": peer, "tp": t}, device_id_type=MESH)
    pl.semaphore_signal(barrier, inc=1, device_id={"ctx": c, "tp": other}, device_id_type=MESH)
    pl.semaphore_wait(barrier, len(peers) + 1)

    put(looked, looked_far, r_look, c, other)
    for far in line:
        to = far * 2 + y
        put(k.at[:, cols(far, HD)], kg.at[c], r_k.at[c], to, t)
        put(v.at[:, cols(far, HD)], vg.at[c], r_v.at[c], to, t)
        put(q.at[:, cols(far, HD)], qg.at[z], r_q.at[z], to, t)
    put(k.at[:, cols(z, HD)], kg.at[c], r_k.at[c], mate, t)
    put(v.at[:, cols(z, HD)], vg.at[c], r_v.at[c], mate, t)
    put(wo.at[:, cols(c, width)], wo_all.at[cols(t, wo.shape[0])], r_wo, c, other)
    fetches = [
        fetch(wo.at[:, cols(c, width)], wo_all.at[cols(t, wo.shape[0])], fetched.at[0]),
        fetch(ein.at[:, cols(c, width)], ein_all.at[y * 4 + z], fetched.at[1]),
        fetch(wk_far, wk, fetched.at[2]),
        fetch(wv_far, wv, fetched.at[3]),
        fetch(wout_far, wout, fetched.at[4]),
    ]
    kg[c] = k[:, cols(z, HD)]
    vg[c] = v[:, cols(z, HD)]
    qg[z] = q[:, cols(z, HD)]

    got(looked_far, r_look)
    hidden = looked[...].astype(F32) + looked_far[...].astype(F32)
    hidden_ref[...] = hidden
    scaled = (hidden * dec_gain[...].astype(F32)).astype(BF16)
    inner = wq.shape[1]
    raw_own[:, :inner] = jnp.dot(scaled, wq[...], preferred_element_type=F32)
    raw_own[:, inner:] = jnp.broadcast_to(
        jnp.sum(hidden * hidden, axis=-1, keepdims=True), (hidden.shape[0], 128)
    )
    share = hidden.shape[0] // 8
    for j in range(8):
        raw_out[j] = raw_own[j * share : (j + 1) * share, :]
    for peer in peers:
        put(raw_out.at[peer], raw_in.at[c], r_raw.at[c], peer, t)
    raw_in[c] = raw_out[c]

    for far in line:
        source = far * 2 + y
        got(kg.at[source], r_k.at[source])
        put(kg.at[source], kg.at[source], r_k.at[source], mate, t)
        got(vg.at[source], r_v.at[source])
        put(vg.at[source], vg.at[source], r_v.at[source], mate, t)
    half = rows // 2
    for peer in peers:
        put(
            ein.at[cols(t, half), cols(peer, width)],
            ein_all.at[y * 4 + z, cols(t, half)],
            r_ein.at[c], peer, t,
        )
    for far in line:
        got(qg.at[far], r_q.at[far])
    for far in range(4):
        source = far * 2 + 1 - y
        got(kg.at[source], r_k.at[source])
        got(vg.at[source], r_v.at[source])

    def block(core, head, side, chunk):
        size = 4 * rows // CHUNKS
        place = ctx_all.at[side, pl.ds(chunk * size, size), cols(core * 4 + head, HD)]
        return place, r_ctx.at[(core * 4 + head) * 2 + side, chunk]

    every_key = kg[...].reshape(8 * rows, HD)
    every_value = vg[...].reshape(8 * rows, HD)
    valid = valid_enc[...] > 0.0
    for chunk in range(CHUNKS):
        some = 4 // CHUNKS
        queries = qg[chunk * some : (chunk + 1) * some].reshape(some * rows, HD)
        scores = lax.dot_general(
            queries, every_key, (((1,), (1,)), ((), ())), preferred_element_type=F32
        ) * (HD ** (-0.5))
        scores = jnp.where(valid, scores, FLOOR)
        top = jnp.max(scores, axis=-1, keepdims=True)
        probs = jnp.where(valid, jnp.exp(scores - top), 0.0)
        total = jnp.sum(probs, axis=-1, keepdims=True)
        mixed = jnp.dot(probs.astype(BF16), every_value, preferred_element_type=F32)
        ctx_all[y, pl.ds(chunk * some * rows, some * rows), cols(t * 4 + z, HD)] = (mixed / total).astype(BF16)
        place, arrival = block(t, z, y, chunk)
        for far in line:
            put(place, place, arrival, far * 2 + y, t)
        put(place, place, arrival, mate, t)
        put(place, place, arrival, c, other)

    for peer in peers:
        got(raw_in.at[peer], r_raw.at[peer])
    raw = raw_in[0]
    for j in range(1, 8):
        raw = raw + raw_in[j]
    factor = lax.rsqrt(raw[:, inner : inner + 1] / D + EPSILON)
    query_in[c] = (raw[:, :inner] * factor * HD ** (-0.5)).astype(BF16).astype(F32)
    for peer in peers:
        put(query_in.at[c], query_in.at[c], r_query.at[c], peer, t)

    for peer in peers:
        place = ein_all.at[lax.rem(peer, 2) * 4 + lax.div(peer, 2), cols(t, half)]
        got(place, r_ein.at[peer])
        put(place, place, r_ein_far.at[peer], c, other)
    for chunk in range(CHUNKS):
        for far in line:
            place, arrival = block(t, far, y, chunk)
            got(place, arrival)
            put(place, place, arrival, mate, t)
            put(place, place, arrival, c, other)
    for chunk in range(CHUNKS):
        for far in range(4):
            place, arrival = block(t, far, 1 - y, chunk)
            got(place, arrival)
            put(place, place, arrival, c, other)
    got(wo_all.at[cols(other, wo.shape[0])], r_wo)
    for peer in peers:
        place = ein_all.at[lax.rem(peer, 2) * 4 + lax.div(peer, 2), cols(other, half)]
        got(place, r_ein_far.at[peer])
    for copy in fetches:
        copy.wait()

    each = rows // 8
    spot_row = lax.broadcasted_iota(jnp.int32, (rows, rows), 0)
    spot_col = lax.broadcasted_iota(jnp.int32, (rows, rows), 1)
    turn = (spot_col == lax.rem(spot_row, each) * 8 + lax.div(spot_row, each)).astype(BF16)
    picked = lax.broadcasted_iota(jnp.int32, enc_gain.shape, 0) == c
    gain = jnp.sum(jnp.where(picked, enc_gain[...].astype(F32), 0.0), axis=0, keepdims=True)
    squares = jnp.zeros((8, rows), F32)
    for chunk in range(CHUNKS):
        for side in range(2):
            for far in range(4):
                place, arrival = block(other, far, side, chunk)
                got(place, arrival)
        for side in range(2):
            for far in range(chunk * 4 // CHUNKS, (chunk + 1) * 4 // CHUNKS):
                source = far * 2 + side
                resid = jnp.dot(
                    ctx_all[side, far * rows : (far + 1) * rows, :], wo_all[...], preferred_element_type=F32
                ) + ein_all[side * 4 + far].astype(F32)
                spread = jnp.where(
                    spot_col == source * each + lax.div(spot_row, 8),
                    jnp.sum(resid * resid, axis=-1, keepdims=True),
                    0.0,
                )
                squares = squares + jnp.sum(spread.reshape(each, 8, rows), axis=0)
                gained = (resid * gain).astype(BF16)
                moved = jnp.dot(turn, gained, preferred_element_type=F32).astype(BF16)
                for r in range(8):
                    gained_all[r, source * each : (source + 1) * each, :] = moved[r * each : (r + 1) * each]
    for r in range(8):
        square_out[r] = squares[r : r + 1]

    def at_ring(place):
        place = lax.rem(place + 16, 8)
        return jnp.where(place < 4, place * 2, (7 - place) * 2 + 1)

    spot = z + y * (7 - 2 * z)
    piece = rows // SUBS
    ways = ((part_k, slot_k, 1, wk), (part_v, slot_v, -1, wv))

    def term(hop):
        for part, slot, step, weight in ways:
            own = gained_all[at_ring(spot - step * (hop + 1))]
            part[hop] = jnp.dot(own, weight[...], preferred_element_type=F32).astype(BF16)

    term(0)
    for sub in range(SUBS):
        lines = pl.ds(sub * piece, piece)
        for way, (part, slot, step, weight) in enumerate(ways):
            put(
                part.at[0, lines], slot.at[0, lines],
                r_ring.at[way, 0, sub], at_ring(spot + step), t,
            )
    for peer in peers:
        put(square_out.at[peer], square_in.at[c], r_square.at[c], peer, t)
    square_in[c] = square_out[c]
    for peer in peers:
        got(query_in.at[peer], r_query.at[peer])
    for j in range(8):
        query_all[j * share : (j + 1) * share, :] = query_in[j]
    for peer in peers:
        got(square_in.at[peer], r_square.at[peer])
    square = square_in[0]
    for j in range(1, 8):
        square = square + square_in[j]
    column = jnp.sum(jnp.where(spot_row == spot_col, square, 0.0), axis=-1, keepdims=True)
    scale = lax.rsqrt(column / D + EPSILON)

    term(1)
    for hop in range(7):
        for sub in range(SUBS):
            lines = pl.ds(sub * piece, piece)
            for way, (part, slot, step, weight) in enumerate(ways):
                got(slot.at[hop, lines], r_ring.at[way, hop, sub])
                here = part[hop + 1, lines].astype(F32)
                running = slot[hop, lines].astype(F32) + here
                if hop < 6:
                    slot[hop, lines] = running.astype(BF16)
                    put(
                        slot.at[hop, lines], slot.at[hop + 1, lines],
                        r_ring.at[way, hop + 1, sub], at_ring(spot + step), t,
                    )
                else:
                    out = keys_out if way == 0 else values_out
                    out[lines] = (running * scale[sub * piece : (sub + 1) * piece]).astype(BF16)
        if hop < 6:
            term(hop + 2)

    own_valid = valid_dec[...] > 0.0
    lanes = lax.broadcasted_iota(jnp.int32, stats_out.shape, 1)
    stats = jnp.zeros(stats_out.shape, F32)
    heads = inner // HD
    for head in range(heads):
        part = slice(head * HD, (head + 1) * HD)
        scores = lax.dot_general(
            query_all[:, part].astype(BF16), keys_out[:, part], (((1,), (1,)), ((), ())),
            preferred_element_type=F32,
        )
        scores = jnp.where(own_valid, scores, FLOOR)
        top = jnp.max(scores, axis=-1, keepdims=True)
        probs = jnp.where(own_valid, jnp.exp(scores - top), 0.0)
        stats = jnp.where(lanes == head, top, stats)
        stats = jnp.where(lanes == heads + head, jnp.sum(probs, axis=-1, keepdims=True), stats)
        mixed_out[:, part] = jnp.dot(
            probs.astype(BF16), values_out[:, part], preferred_element_type=F32
        ).astype(BF16)
    stats_out[...] = stats
    for peer in peers:
        put(stats_out, stats_in.at[c], r_stats.at[c], peer, t)
        put(mixed_out, mixed_in.at[c], r_mixed.at[c], peer, t)
    stats_in[c] = stats_out[...]
    mixed_in[c] = mixed_out[...]
    for peer in peers:
        got(stats_in.at[peer], r_stats.at[peer])
        got(mixed_in.at[peer], r_mixed.at[peer])
    proj = jnp.zeros(proj_out.shape, F32)
    for head in range(heads):
        part = slice(head * HD, (head + 1) * HD)
        tops = [stats_in[j][:, head : head + 1] for j in range(8)]
        top = tops[0]
        for j in range(1, 8):
            top = jnp.maximum(top, tops[j])
        total = jnp.zeros_like(top)
        mixed = jnp.zeros((top.shape[0], HD), F32)
        for j in range(8):
            weight = jnp.exp(tops[j] - top)
            total = total + stats_in[j][:, heads + head : heads + head + 1] * weight
            mixed = mixed + mixed_in[j][:, part].astype(F32) * weight
        proj = proj + jnp.dot((mixed / total).astype(BF16), wout[part, :], preferred_element_type=F32)
    proj_out[...] = proj
    put(proj_out, proj_in, r_proj, c, other)
    got(proj_in, r_proj)
    decoded_out[...] = proj_out[...] + proj_in[...] + hidden_ref[...]
    for copy in pending:
        copy.wait_send()


def local_fused(
    enc_input, enc_query, enc_key, enc_value, seq_length, attn_out_weight, enc_gain, cross_key_weight,
    cross_value_weight, embed_table, dec_ids, dec_gain, cross_query_weight, cross_out_weight,
):
    rows, inner = enc_query.shape
    width = cross_query_weight.shape[0]
    tokens = dec_ids.size
    whole = pl.BlockSpec(memory_space=pltpu.VMEM)
    scalars = pl.BlockSpec(memory_space=pltpu.SMEM)
    anywhere = pl.BlockSpec(memory_space=pl.ANY)
    looked, valid_enc, valid_dec = pl.pallas_call(
        pick_kernel,
        out_shape=(
            jax.ShapeDtypeStruct((tokens, width), BF16),
            jax.ShapeDtypeStruct((1, 8 * rows), F32),
            jax.ShapeDtypeStruct((1, rows), F32),
        ),
        in_specs=[scalars, scalars, anywhere],
        out_specs=(whole, whole, whole),
        scratch_shapes=[
            pltpu.VMEM((tokens, 16, width), BF16),
            pltpu.VMEM((tokens, width), F32),
            pltpu.SemaphoreType.DMA((tokens,)),
        ],
    )(dec_ids.reshape(-1), seq_length, embed_table)
    dma = pltpu.SemaphoreType.DMA
    share = tokens // 8
    keys, values, decoded = pl.pallas_call(
        fused_kernel,
        out_shape=(
            jax.ShapeDtypeStruct((rows, inner), BF16),
            jax.ShapeDtypeStruct((rows, inner), BF16),
            jax.ShapeDtypeStruct((tokens, width), F32),
        ),
        in_specs=[
            whole, whole, whole, anywhere, whole, whole, whole, anywhere, whole, anywhere, anywhere, anywhere,
            whole, whole,
        ],
        out_specs=(whole, whole, whole),
        scratch_shapes=[
            pltpu.VMEM((tokens, width), BF16),
            pltpu.VMEM((2 * inner, width), BF16),
            pltpu.VMEM((4, rows, HD), BF16),
            pltpu.VMEM((8, rows, HD), BF16),
            pltpu.VMEM((8, rows, HD), BF16),
            pltpu.VMEM((8, rows, width), BF16),
            pltpu.VMEM((2, 4 * rows, 2 * inner), BF16),
            pltpu.VMEM((tokens, inner + 128), F32),
            pltpu.VMEM((8, share, inner + 128), F32),
            pltpu.VMEM((8, share, inner + 128), F32),
            pltpu.VMEM((8, share, inner), F32),
            pltpu.VMEM((tokens, inner), F32),
            pltpu.VMEM((width, inner), BF16),
            pltpu.VMEM((width, inner), BF16),
            pltpu.VMEM((inner, width), BF16),
            pltpu.VMEM((8, rows, width), BF16),
            pltpu.VMEM((8, rows, inner), BF16),
            pltpu.VMEM((8, rows, inner), BF16),
            pltpu.VMEM((7, rows, inner), BF16),
            pltpu.VMEM((7, rows, inner), BF16),
            pltpu.VMEM((8, 1, rows), F32),
            pltpu.VMEM((8, 1, rows), F32),
            pltpu.VMEM((tokens, inner), BF16),
            pltpu.VMEM((8, tokens, inner), BF16),
            pltpu.VMEM((tokens, 128), F32),
            pltpu.VMEM((8, tokens, 128), F32),
            pltpu.VMEM((tokens, width), F32),
            pltpu.VMEM((tokens, width), F32),
            pltpu.VMEM((tokens, width), F32),
            dma, dma, dma, dma((4,)), dma((8,)), dma((8,)), dma((8,)), dma((8,)), dma((8,)), dma((8,)),
            dma((16, CHUNKS)), dma((8,)), dma((2, 7, SUBS)), dma((8,)), dma((8,)), dma, dma((5,)),
        ],
        compiler_params=pltpu.CompilerParams(
            collective_id=0, has_side_effects=True, vmem_limit_bytes=60 * 1024 * 1024
        ),
    )(
        enc_query, enc_key, enc_value, enc_input, looked, dec_gain[None], cross_query_weight, attn_out_weight,
        enc_gain.reshape(8, width),
        cross_key_weight, cross_value_weight, cross_out_weight, valid_enc, valid_dec,
    )
    return pl.pallas_call(
        hand_kernel,
        out_shape=(
            jax.ShapeDtypeStruct((1, rows, inner), BF16),
            jax.ShapeDtypeStruct((1, rows, inner), BF16),
            jax.ShapeDtypeStruct((tokens // 2, 2, width), BF16),
        ),
        in_specs=[whole] * 3,
        out_specs=(whole, whole, whole),
    )(keys, values, decoded)


def chosen(*arrays):
    rows, inner = arrays[1].shape
    fits = lax.axis_size("ctx") == 8 and lax.axis_size("tp") == 2 and (rows, inner) == (128, 4 * HD)
    return (local_fused if fits else local)(*arrays)


def solution(mesh):
    placed = (
        P(("groups", "ctx"), None),
        P(("groups", "ctx"), "tp"),
        P(("groups", "ctx"), "tp"),
        P(("groups", "ctx"), "tp"),
        P("groups"),
        P("tp", None),
        P(),
        P("ctx", "tp"),
        P("ctx", "tp"),
        P("tp", "ctx"),
        P("groups", None),
        P("ctx"),
        P("ctx", "tp"),
        P("tp", "ctx"),
    )
    return jax.shard_map(
        chosen,
        mesh=mesh,
        in_specs=placed,
        out_specs=(
            P(("groups", "ctx"), None, "tp"),
            P(("groups", "ctx"), None, "tp"),
            P("groups", None, "ctx"),
        ),
        check_vma=False,
    )
```

profile of v0, /device:TPU:0, one launch (start us, length us, event | category | flops | bytes accessed | tf_op | source)
XLA Modules:
  0.0 100.4 jit_solution(13473319302442875019)
XLA Ops:
  1.3 1.2 %broadcast_in_dim.3.dec_gain = bf16[1,512]{1,0:T(2,128)(2,1)} reshape(bf16[512]{0:T(512)(128)(2,1)} %param.25) | data formatting | bytes 2048 | tf_op jit(solution)/shard_map/broadcast_in_dim | solution.py:582
  2.5 1.3 %reshape.13.enc_gain = bf16[8,512]{1,0:T(8,128)(2,1)} reshape(bf16[4096]{0:T(1024)(128)(2,1)} %param.20) | data formatting | bytes 16384 | tf_op jit(solution)/shard_map/reshape | solution.py:583
  3.8 0.8 copy.18
  4.6 0.6 reshape.12.ids_ref
  5.2 3.1 %shard_map.157 = (bf16[32,512]{1,0:T(8,128)(2,1)}, f32[1,1024]{1,0:T(1,128)}, f32[1,128]{1,0:T(1,128)}) custom-call(s32[32]{0:T(128)} %reshape.12.ids_ref, s32[1]{0:T(128)S(6)} %copy.19.length_ref, bf16[16064,512]{1,0:T(8,128)(2,1)} %table_ref.1), custom_call_target="tpu_custom_call" | custom-call | tf_op jit(solution)/shard_map/pallas_call | solution.py:516
  8.3 90.3 %shard_map.158 = (bf16[128,512]{1,0:T(8,128)(2,1)}, bf16[128,512]{1,0:T(8,128)(2,1)}, f32[32,512]{1,0:T(8,128)}) custom-call(bf16[128,512]{1,0:T(8,128)(2,1)} %q.1, bf16[128,512]{1,0:T(8,128)(2,1)} %k.1, bf16[128,512]{1,0:T(8,128)(2,1)} %v.1, bf16[128,4096]{1,0:T(8,128)(2,1)} %ein.1, bf16[32,512]{1,0:T(8,128)(2,1)} %get-tuple-element.9.looked, ...), custom_call_target="tpu_custom_call" | custom-call | tf_op jit(solution)/shard_map/pallas_call | solution.py:533
  98.7 1.7 %shard_map.159 = (bf16[1,128,512]{2,1,0:T(8,128)(2,1)}, bf16[1,128,512]{2,1,0:T(8,128)(2,1)}, bf16[16,2,512]{2,1,0:T(2,128)(2,1)}) custom-call(bf16[128,512]{1,0:T(8,128)(2,1)} %get-tuple-element.12.keys_ref, bf16[128,512]{1,0:T(8,128)(2,1)} %get-tuple-element.13.values_ref, f32[32,512]{1,0:T(8,128)} %get-tuple-element.14.decoded_ref), custom_call_target="tpu_custom_call" | custom-call | tf_op jit(solution)/shard_map/pallas_call | solution.py:586
where the time goes:
time: 101 us; the launch traced here: 100 us
  Pallas kernels  95.1 us (94%)
  local copies, waits for them, and re-layouts  3.94 us (4%)
  between operations  1.29 us (1%)
    pallas_call x1, Pallas kernels, local_fused(): pl.pallas_call(fused_kernel, out_shape=(jax.ShapeDtypeStruct((rows, inner...  90.3 us
    pallas_call x1, Pallas kernels, local_fused(): pl.pallas_call(pick_kernel, out_shape=(jax.ShapeDtypeStruct((tokens, widt...  3.12 us

commit v1 on v0

v1 whole, which is shorter than its diff:
```python
import math

import jax
import jax.numpy as jnp
from jax import lax
from jax.experimental import pallas as pl
from jax.experimental.pallas import tpu as pltpu
from jax.sharding import PartitionSpec as P

D = 4096
HD = 128


EPSILON = 1e-06
FLOOR = -1e30


def joined(value, axis, join):
    pieces = jax.tree.map(lambda part: lax.all_gather(part, axis), value)
    head = jax.tree.map(lambda part: part[0], pieces)
    tail = jax.tree.map(lambda part: part[1:], pieces)
    total, _ = lax.scan(lambda total, piece: (join(total, piece), None), head, tail)
    return total


def softmax_merge(first, second):
    top_first, total_first, mixed_first = first
    top_second, total_second, mixed_second = second
    top = jnp.maximum(top_first, top_second)
    weight_first = jnp.exp(top_first - top)
    weight_second = jnp.exp(top_second - top)
    total = total_first * weight_first + total_second * weight_second
    mixed = mixed_first * weight_first[..., None] + mixed_second * weight_second[..., None]
    return (top, total, mixed)


def partial_softmax(queries, keys, values, valid, factor):
    scores = jnp.einsum("qhd,khd->hqk", queries, keys, preferred_element_type=jnp.float32) * factor
    scores = jnp.where(valid[None, None, :], scores, FLOOR)
    top = jnp.max(scores, axis=-1)
    probs = jnp.where(valid[None, None, :], jnp.exp(scores - top[..., None]), 0.0)
    total = jnp.sum(probs, axis=-1)
    mixed = jnp.einsum(
        "hqk,khd->hqd", probs.astype(jnp.bfloat16), values, preferred_element_type=jnp.float32
    )
    return (top, total, mixed)


def norm_rows(resid, gain):
    scale = lax.rsqrt(jnp.mean(resid * resid, axis=-1, keepdims=True) + EPSILON)
    return (resid * scale * gain.astype(jnp.float32)).astype(jnp.bfloat16)


def local(
    enc_input,
    enc_query,
    enc_key,
    enc_value,
    seq_length,
    attn_out_weight,
    enc_gain,
    cross_key_weight,
    cross_value_weight,
    embed_table,
    dec_ids,
    dec_gain,
    cross_query_weight,
    cross_out_weight,
):
    rows, inner_local = enc_query.shape
    heads_local = inner_local // HD
    limit = seq_length[0]
    queries = enc_query.reshape(rows, heads_local, HD)
    start_state = (
        jnp.full((heads_local, rows), FLOOR, jnp.float32),
        jnp.zeros((heads_local, rows), jnp.float32),
        jnp.zeros((heads_local, rows, HD), jnp.float32),
    )
    carry = start_state
    key_rows = lax.all_gather(enc_key, "ctx", axis=0, tiled=True)
    value_rows = lax.all_gather(enc_value, "ctx", axis=0, tiled=True)
    count = key_rows.shape[0]
    block = math.gcd(count, 2048)
    blocks = count // block
    key_blocks = key_rows.reshape(blocks, block, heads_local, HD)
    value_blocks = value_rows.reshape(blocks, block, heads_local, HD)
    offsets = jnp.arange(blocks, dtype=jnp.int32) * block

    def one_block(state, item):
        key_block, value_block, offset = item
        positions = offset + jnp.arange(block, dtype=jnp.int32)
        update = partial_softmax(queries, key_block, value_block, positions < limit, HD ** (-0.5))
        return (softmax_merge(state, update), None)

    carry, unused = lax.scan(one_block, carry, (key_blocks, value_blocks, offsets))
    top, total, mixed = carry
    context = (
        jnp.transpose(mixed / total[..., None], (1, 0, 2))
        .reshape(rows, inner_local)
        .astype(jnp.bfloat16)
    )
    summed = lax.psum(jnp.dot(context, attn_out_weight, preferred_element_type=jnp.float32), "tp")
    memory = norm_rows(enc_input.astype(jnp.float32) + summed, enc_gain)
    ctx_count = lax.axis_size("ctx")
    slots = rows // ctx_count
    key_sum = jnp.dot(
        memory,
        lax.all_gather(cross_key_weight, "ctx", axis=0, tiled=True),
        preferred_element_type=jnp.float32,
    )
    value_sum = jnp.dot(
        memory,
        lax.all_gather(cross_value_weight, "ctx", axis=0, tiled=True),
        preferred_element_type=jnp.float32,
    )
    key_rows = key_sum.astype(jnp.bfloat16)
    value_rows = value_sum.astype(jnp.bfloat16)
    keys_moved, values_moved = (
        lax.all_to_all(
            key_rows.reshape(slots, ctx_count, inner_local),
            "ctx",
            split_axis=1,
            concat_axis=0,
            tiled=True,
        ),
        lax.all_to_all(
            value_rows.reshape(slots, ctx_count, inner_local),
            "ctx",
            split_axis=1,
            concat_axis=0,
            tiled=True,
        ),
    )
    keys_cache = keys_moved.reshape(rows, inner_local)
    values_cache = values_moved.reshape(rows, inner_local)
    beams = dec_ids.shape[0]
    vocab_local = embed_table.shape[0]
    flat_ids = dec_ids.reshape(-1) - lax.axis_index("tp") * vocab_local
    inside = (flat_ids >= 0) & (flat_ids < vocab_local)
    looked = jnp.take(embed_table, jnp.clip(flat_ids, 0, vocab_local - 1), axis=0)
    own_rows = jnp.where(inside[:, None], looked.astype(jnp.float32), 0.0)
    hidden = lax.psum(own_rows.astype(jnp.bfloat16), "tp").astype(jnp.float32)
    scaled = (hidden * dec_gain.astype(jnp.float32)).astype(jnp.bfloat16)
    raw_part = jnp.dot(scaled, cross_query_weight, preferred_element_type=jnp.float32)
    square_part = jnp.sum(hidden * hidden, axis=-1)
    raw, squares = lax.psum((raw_part, square_part), "ctx")
    factor = lax.rsqrt(squares / D + EPSILON)
    query = (raw * factor[:, None] * HD ** (-0.5)).astype(jnp.bfloat16).reshape(-1, heads_local, HD)
    positions = jnp.arange(rows, dtype=jnp.int32) * ctx_count + lax.axis_index("ctx")
    local_part = partial_softmax(
        query,
        keys_cache.reshape(rows, heads_local, HD),
        values_cache.reshape(rows, heads_local, HD),
        positions < limit,
        1.0,
    )
    top_all, total_all, mixed_all = joined(local_part, "ctx", softmax_merge)
    attn = (
        jnp.transpose(mixed_all / total_all[..., None], (1, 0, 2))
        .reshape(-1, inner_local)
        .astype(jnp.bfloat16)
    )
    out_part = jnp.dot(attn, cross_out_weight, preferred_element_type=jnp.float32)
    out = lax.psum(out_part, "tp")
    decoded = (out + hidden).astype(jnp.bfloat16).reshape(beams, 2, -1)
    return (keys_cache[None], values_cache[None], decoded)


MESH = pl.DeviceIdType.MESH
F32 = jnp.float32
BF16 = jnp.bfloat16
ORDER = (3, 0, 2, 1)


def pick_kernel(ids_ref, table_ref, out_ref, held, rows, sems):
    count = out_ref.shape[0]
    vocab_local = table_ref.shape[0]
    base = lax.axis_index("tp") * vocab_local
    copies = []
    for j in range(count):
        own = jnp.clip(ids_ref[j % 2, j // 2] - base, 0, vocab_local - 1)
        start = pl.multiple_of(lax.div(own, 16) * 16, 16)
        copy = pltpu.make_async_copy(table_ref.at[pl.ds(start, 16)], held.at[j], sems.at[j])
        copy.start()
        copies.append(copy)
    spots = lax.broadcasted_iota(jnp.int32, held.shape[1:], 0)
    for j in range(count):
        copies[j].wait()
        own = ids_ref[j % 2, j // 2] - base
        inside = (own >= 0) & (own < vocab_local)
        spot = jnp.where(inside, lax.rem(jnp.clip(own, 0, vocab_local - 1), 16), -1)
        block = held[j].astype(F32)
        rows[pl.ds(j, 1)] = jnp.sum(jnp.where(spots == spot, block, 0.0), axis=0, keepdims=True)
    out_ref[...] = rows[...].astype(BF16)


def hand_kernel(keys_ref, values_ref, decoded_ref, keys_out, values_out, decoded_out):
    keys_out[0] = keys_ref[...]
    values_out[0] = values_ref[...]
    for i in range(decoded_out.shape[0]):
        decoded_out[i] = decoded_ref[2 * i : 2 * i + 2].astype(BF16)


def fused_kernel(
    length, gains, q, k, v, ein, looked_hbm, wq, wo, wk, wv, wout,
    keys_out, values_out, decoded_out,
    q_own, q_turned, ein_own, ein_turned, looked, looked_far, wq_own, wout_own,
    kg, vg, qg, eg, wo_all, wk_all, wv_all, ctx_all, gained, square_own, square_far, square_sum, square_in,
    part_k, part_v, pair_k, pair_v, near_k, near_v, far_k, far_v, keys_own, values_own,
    raw_own, raw_out, raw_in, query_in, query_all, mix_own, mix_out, mix_in, attn_in, attn_all, proj_out, proj_in, hidden_ref,
    send, r_look, r_wo, r_q, r_k, r_v, r_wk, r_wv, r_raw, r_query, r_ein, r_ctx, r_gained, r_square_far, r_square,
    r_pair, r_near, r_far, r_mix, r_attn, r_proj, fetched, stored,
):
    c = lax.axis_index("ctx")
    t = lax.axis_index("tp")
    z, y = lax.div(c, 2), lax.rem(c, 2)
    mate, other = c + 1 - 2 * y, 1 - t
    line = [lax.rem(z + d, 4) for d in (2, 1, 3)]
    peers = [lax.rem(c + d, 8) for d in range(1, 8)]
    rows = q.shape[0]
    inner = q.shape[1]
    width = wq.shape[0]
    half = rows // 2
    each = rows // 8
    own_block = z * 2 + t
    heads = inner // HD
    pending = []

    def remote(source, target, arrival, to_ctx, to_tp):
        return pltpu.make_async_remote_copy(
            src_ref=source, dst_ref=target, send_sem=send, recv_sem=arrival,
            device_id={"ctx": to_ctx, "tp": to_tp}, device_id_type=MESH,
        )

    def put(source, target, arrival, to_ctx, to_tp):
        copy = remote(source, target, arrival, to_ctx, to_tp)
        copy.start()
        pending.append(copy)

    def got(target, arrival):
        remote(target, target, arrival, mate, t).wait_recv()

    def fetch(source, target, arrival):
        copy = pltpu.make_async_copy(source, target, arrival)
        copy.start()
        return copy

    def cols(index, size):
        return pl.ds(pl.multiple_of(index * size, size), size)

    barrier = pltpu.get_barrier_semaphore()
    for peer in peers:
        pl.semaphore_signal(barrier, inc=1, device_id={"ctx": peer, "tp": t}, device_id_type=MESH)
    pl.semaphore_signal(barrier, inc=1, device_id={"ctx": c, "tp": other}, device_id_type=MESH)

    q_fetch = fetch(q, q_own, fetched.at[0])
    k_fetch = fetch(k.at[:, cols(z, HD)], kg.at[c], fetched.at[1])
    v_fetch = fetch(v.at[:, cols(z, HD)], vg.at[c], fetched.at[2])
    ein_fetches = [
        fetch(ein.at[:, cols(far * 2 + t, width)], ein_own.at[far], fetched.at[3 + far]) for far in range(4)
    ]
    looked_fetch = fetch(looked_hbm, looked, fetched.at[7])
    wq_fetch = fetch(wq, wq_own, fetched.at[8])
    late = [
        fetch(wo.at[:, cols(own_block, width)], wo_all.at[cols(t, inner)], fetched.at[9]),
        fetch(wk, wk_all.at[y], fetched.at[10]),
        fetch(wv, wv_all.at[y], fetched.at[11]),
    ]
    wout_fetch = fetch(wout, wout_own, fetched.at[12])
    pl.semaphore_wait(barrier, len(peers) + 1)

    for far in line:
        to = far * 2 + y
        put(k.at[:, cols(far, HD)], kg.at[c], r_k.at[c], to, t)
        put(v.at[:, cols(far, HD)], vg.at[c], r_v.at[c], to, t)
    put(k.at[:, cols(z, HD)], kg.at[c], r_k.at[c], mate, t)
    put(v.at[:, cols(z, HD)], vg.at[c], r_v.at[c], mate, t)

    place = lax.broadcasted_iota(jnp.int32, (rows, rows), 0)
    spot = lax.broadcasted_iota(jnp.int32, (rows, rows), 1)
    side, rest = lax.div(place, half), lax.rem(place, half)
    turn = (spot == lax.rem(rest, each) * 8 + lax.div(rest, each) * 2 + side).astype(BF16)

    q_fetch.wait()
    turned = jnp.dot(turn, q_own[...], preferred_element_type=F32).astype(BF16)
    for s in range(2):
        q_turned[s] = turned[s * half : (s + 1) * half]
    for peer in peers:
        put(
            q_turned.at[lax.rem(peer, 2), :, cols(lax.div(peer, 2), HD)], qg.at[c], r_q.at[c], peer, t
        )
    qg[c] = q_turned[y, :, cols(z, HD)]
    put(wo.at[:, cols(z * 2 + other, width)], wo_all.at[cols(t, inner)], r_wo, c, other)

    for far in range(4):
        ein_fetches[far].wait()
        turned = jnp.dot(turn, ein_own[far], preferred_element_type=F32).astype(BF16)
        for s in range(2):
            ein_turned[far, s] = turned[s * half : (s + 1) * half]

    for far in line:
        source = far * 2 + y
        got(kg.at[source], r_k.at[source])
        put(kg.at[source], kg.at[source], r_k.at[source], mate, t)
        got(vg.at[source], r_v.at[source])
        put(vg.at[source], vg.at[source], r_v.at[source], mate, t)
    for peer in peers:
        put(ein_turned.at[lax.div(peer, 2), lax.rem(peer, 2)], eg.at[c], r_ein.at[c], peer, t)
    eg[c] = ein_turned[z, y]
    put(wk, wk_all.at[y], r_wk, mate, t)
    put(wv, wv_all.at[y], r_wv, mate, t)

    tokens = looked.shape[0]
    looked_fetch.wait()
    put(looked, looked_far, r_look, c, other)

    k_fetch.wait()
    v_fetch.wait()
    for peer in peers:
        got(qg.at[peer], r_q.at[peer])
    for far in range(4):
        source = far * 2 + 1 - y
        got(kg.at[source], r_k.at[source])
        got(vg.at[source], r_v.at[source])

    limit = length[0]
    every_key = kg[...].reshape(8 * rows, HD)
    every_value = vg[...].reshape(8 * rows, HD)
    valid = lax.broadcasted_iota(jnp.int32, (1, 8 * rows), 1) < limit

    def block_at(core, far, chunk):
        return ctx_all.at[chunk, :, cols(core * 4 + far, HD)], r_ctx.at[core * 4 + far, chunk]

    for chunk in ORDER:
        queries = qg[:, chunk * each : (chunk + 1) * each, :].reshape(rows, HD)
        scores = lax.dot_general(
            queries, every_key, (((1,), (1,)), ((), ())), preferred_element_type=F32
        ) * (HD ** (-0.5))
        scores = jnp.where(valid, scores, FLOOR)
        top = jnp.max(scores, axis=-1, keepdims=True)
        probs = jnp.where(valid, jnp.exp(scores - top), 0.0)
        total = jnp.sum(probs, axis=-1, keepdims=True)
        mixed = jnp.dot(probs.astype(BF16), every_value, preferred_element_type=F32)
        ctx_all[chunk, :, cols(t * 4 + z, HD)] = (mixed / total).astype(BF16)
        here, arrival = block_at(t, z, chunk)
        for far in line:
            put(here, here, arrival, far * 2 + y, t)
        put(here, here, arrival, c, other)

    got(looked_far, r_look)
    wq_fetch.wait()
    hidden = looked[...].astype(F32) + looked_far[...].astype(F32)
    hidden_ref[...] = hidden
    scaled = (hidden * gains[0:1]).astype(BF16)
    raw_own[:, :inner] = jnp.dot(scaled, wq_own[...], preferred_element_type=F32)
    raw_own[:, inner:] = jnp.broadcast_to(jnp.sum(hidden * hidden, axis=-1, keepdims=True), (tokens, 128))
    share = tokens // 8
    for j in range(8):
        raw_out[j] = raw_own[j * share : (j + 1) * share, :]
    for peer in peers:
        put(raw_out.at[peer], raw_in.at[c], r_raw.at[c], peer, t)
    raw_in[c] = raw_out[c]

    for copy in late:
        copy.wait()
    got(wo_all.at[cols(other, inner)], r_wo)
    for peer in peers:
        got(eg.at[peer], r_ein.at[peer])
    picked_gain = lax.broadcasted_iota(jnp.int32, (8, width), 0) == own_block
    gain = jnp.sum(jnp.where(picked_gain, gains[8:16], 0.0), axis=0, keepdims=True)

    def relay(chunk):
        for far in line:
            here, arrival = block_at(t, far, chunk)
            got(here, arrival)
            put(here, here, arrival, c, other)

    def project(chunk):
        for far in range(4):
            got(*block_at(other, far, chunk))
        resid = jnp.dot(ctx_all[chunk], wo_all[...], preferred_element_type=F32)
        resid = resid + eg[:, chunk * each : (chunk + 1) * each, :].reshape(rows, width).astype(F32)
        spread = jnp.where(place == spot, jnp.sum(resid * resid, axis=-1, keepdims=True), 0.0)
        square_own[chunk] = jnp.sum(spread, axis=0, keepdims=True)
        gained[chunk, t] = (resid * gain).astype(BF16)
        put(gained.at[chunk, t], gained.at[chunk, t], r_gained.at[chunk], c, other)
        put(square_own.at[chunk], square_far.at[chunk], r_square_far.at[chunk], c, other)

    ways = ((part_k, pair_k, near_k, far_k, wk_all, r_wk), (part_v, pair_v, near_v, far_v, wv_all, r_wv))

    def start_only(source, target, arrival, to_z):
        remote(source, target, arrival, to_z * 2 + y, t).start()

    def spread_out(chunk, first):
        got(gained.at[chunk, other], r_gained.at[chunk])
        end = 0 if chunk >= 2 else 3
        for way, (part, pair, near, far, weight, arrival) in enumerate(ways):
            if first:
                got(weight.at[1 - y], arrival)
            total = jnp.dot(gained[chunk, 0], weight[0], preferred_element_type=F32)
            total = total + jnp.dot(gained[chunk, 1], weight[1], preferred_element_type=F32)
            part[chunk] = total.astype(BF16)

            @pl.when(z == end)
            def _():
                start_only(
                    part.at[chunk], pair.at[chunk % 2], r_pair.at[way, chunk % 2], 1 if end == 0 else 2
                )

            @pl.when(z == (chunk + 1 if chunk % 2 == 0 else chunk - 1))
            def _():
                start_only(part.at[chunk], near, r_near.at[way], chunk)

    def join(chunk):
        middle = 1 if chunk >= 2 else 2
        for way, (part, pair, near, far, weight, arrival) in enumerate(ways):

            @pl.when(z == middle)
            def _():
                got(pair.at[chunk % 2], r_pair.at[way, chunk % 2])
                both = part[chunk].astype(F32) + pair[chunk % 2].astype(F32)
                pair[chunk % 2] = both.astype(BF16)
                start_only(pair.at[chunk % 2], far, r_far.at[way], chunk)

    relay(ORDER[0])
    relay(ORDER[1])
    project(ORDER[0])
    relay(ORDER[2])
    project(ORDER[1])
    spread_out(ORDER[0], True)
    relay(ORDER[3])
    project(ORDER[2])
    spread_out(ORDER[1], False)
    project(ORDER[3])
    spread_out(ORDER[2], False)
    spread_out(ORDER[3], False)
    for chunk in range(4):
        got(square_far.at[chunk], r_square_far.at[chunk])
        square_sum[chunk] = square_own[chunk] + square_far[chunk]
    for far in line:
        put(square_sum.at[far], square_in.at[z], r_square.at[z], far * 2 + y, t)
    square_in[z] = square_sum[z]

    join(ORDER[0])
    join(ORDER[1])
    for peer in peers:
        got(raw_in.at[peer], r_raw.at[peer])
    raw = raw_in[0]
    for j in range(1, 8):
        raw = raw + raw_in[j]
    factor = lax.rsqrt(raw[:, inner : inner + 1] / D + EPSILON)
    query_in[c] = (raw[:, :inner] * factor * HD ** (-0.5)).astype(BF16).astype(F32)
    for peer in peers:
        put(query_in.at[c], query_in.at[c], r_query.at[c], peer, t)
    join(ORDER[2])
    join(ORDER[3])

    for far in line:
        got(square_in.at[far], r_square.at[far])
    square = square_in[0] + square_in[1] + square_in[2] + square_in[3]
    column = jnp.sum(jnp.where(place == spot, square, 0.0), axis=-1, keepdims=True)
    scale = lax.rsqrt(column / D + EPSILON)
    for peer in peers:
        got(query_in.at[peer], r_query.at[peer])
    for j in range(8):
        query_all[j * share : (j + 1) * share, :] = query_in[j]

    stores = []
    for way, (own, out) in enumerate(((keys_own, keys_out), (values_own, values_out))):
        part, pair, near, far, weight, arrival = ways[way]
        got(near, r_near.at[way])
        got(far, r_far.at[way])
        total = part[z].astype(F32) + near[...].astype(F32) + far[...].astype(F32)
        own[...] = (total * scale).astype(BF16)
        stores.append(fetch(own, out, stored.at[way]))

    own_valid = lax.broadcasted_iota(jnp.int32, (1, rows), 1) * 8 + c < limit
    lanes = lax.broadcasted_iota(jnp.int32, (tokens, 128), 1)
    stats = jnp.zeros((tokens, 128), F32)
    for head in range(heads):
        part = slice(head * HD, (head + 1) * HD)
        scores = lax.dot_general(
            query_all[:, part].astype(BF16), keys_own[:, part], (((1,), (1,)), ((), ())),
            preferred_element_type=F32,
        )
        scores = jnp.where(own_valid, scores, FLOOR)
        top = jnp.max(scores, axis=-1, keepdims=True)
        probs = jnp.where(own_valid, jnp.exp(scores - top), 0.0)
        stats = jnp.where(lanes == head, top, stats)
        stats = jnp.where(lanes == heads + head, jnp.sum(probs, axis=-1, keepdims=True), stats)
        mix_own[:, part] = jnp.dot(probs.astype(BF16), values_own[:, part], preferred_element_type=F32)
    mix_own[:, inner:] = stats
    for j in range(8):
        mix_out[j] = mix_own[j * share : (j + 1) * share, :]
    for peer in peers:
        put(mix_out.at[peer], mix_in.at[c], r_mix.at[c], peer, t)
    mix_in[c] = mix_out[c]
    for peer in peers:
        got(mix_in.at[peer], r_mix.at[peer])
    for head in range(heads):
        part = slice(head * HD, (head + 1) * HD)
        tops = [mix_in[j][:, inner + head : inner + head + 1] for j in range(8)]
        top = tops[0]
        for j in range(1, 8):
            top = jnp.maximum(top, tops[j])
        total = jnp.zeros_like(top)
        mixed = jnp.zeros((share, HD), F32)
        for j in range(8):
            weight = jnp.exp(tops[j] - top)
            total = total + mix_in[j][:, inner + heads + head : inner + heads + head + 1] * weight
            mixed = mixed + mix_in[j][:, part] * weight
        attn_in[c, :, part] = (mixed / total).astype(BF16).astype(F32)
    for peer in peers:
        put(attn_in.at[c], attn_in.at[c], r_attn.at[c], peer, t)
    for peer in peers:
        got(attn_in.at[peer], r_attn.at[peer])
    for j in range(8):
        attn_all[j * share : (j + 1) * share, :] = attn_in[j]
    wout_fetch.wait()
    proj_out[...] = jnp.dot(attn_all[...].astype(BF16), wout_own[...], preferred_element_type=F32)
    put(proj_out, proj_in, r_proj, c, other)
    got(proj_in, r_proj)
    decoded_out[...] = proj_out[...] + proj_in[...] + hidden_ref[...]
    for copy in stores:
        copy.wait()
    for copy in pending:
        copy.wait_send()
    for i in range(6):
        remote(near_k, near_k, r_near.at[0], mate, t).wait_send()


def local_fused(
    enc_input, enc_query, enc_key, enc_value, seq_length, attn_out_weight, enc_gain, cross_key_weight,
    cross_value_weight, embed_table, dec_ids, dec_gain, cross_query_weight, cross_out_weight,
):
    rows, inner = enc_query.shape
    width = cross_query_weight.shape[0]
    tokens = dec_ids.size
    whole = pl.BlockSpec(memory_space=pltpu.VMEM)
    scalars = pl.BlockSpec(memory_space=pltpu.SMEM)
    anywhere = pl.BlockSpec(memory_space=pl.ANY)
    gains = jnp.concatenate(
        [jnp.broadcast_to(dec_gain[None], (8, width)), enc_gain.reshape(8, width)], axis=0
    ).astype(F32)
    dma = pltpu.SemaphoreType.DMA
    share = tokens // 8
    half = rows // 2
    looked = pl.pallas_call(
        pick_kernel,
        out_shape=jax.ShapeDtypeStruct((tokens, width), BF16),
        in_specs=[scalars, anywhere],
        out_specs=whole,
        scratch_shapes=[
            pltpu.VMEM((tokens, 16, width), BF16),
            pltpu.VMEM((tokens, width), F32),
            pltpu.SemaphoreType.DMA((tokens,)),
        ],
    )(dec_ids.T, embed_table)
    keys, values, decoded = pl.pallas_call(
        fused_kernel,
        out_shape=(
            jax.ShapeDtypeStruct((rows, inner), BF16),
            jax.ShapeDtypeStruct((rows, inner), BF16),
            jax.ShapeDtypeStruct((tokens, width), F32),
        ),
        in_specs=[scalars, whole] + [anywhere] * 10,
        out_specs=(anywhere, anywhere, whole),
        scratch_shapes=[
            pltpu.VMEM((rows, inner), BF16),
            pltpu.VMEM((2, half, inner), BF16),
            pltpu.VMEM((4, rows, width), BF16),
            pltpu.VMEM((4, 2, half, width), BF16),
            pltpu.VMEM((tokens, width), BF16),
            pltpu.VMEM((tokens, width), BF16),
            pltpu.VMEM((width, inner), BF16),
            pltpu.VMEM((inner, width), BF16),
            pltpu.VMEM((8, rows, HD), BF16),
            pltpu.VMEM((8, rows, HD), BF16),
            pltpu.VMEM((8, half, HD), BF16),
            pltpu.VMEM((8, half, width), BF16),
            pltpu.VMEM((2 * inner, width), BF16),
            pltpu.VMEM((2, width, inner), BF16),
            pltpu.VMEM((2, width, inner), BF16),
            pltpu.VMEM((4, rows, 2 * inner), BF16),
            pltpu.VMEM((4, 2, rows, width), BF16),
            pltpu.VMEM((4, 1, rows), F32),
            pltpu.VMEM((4, 1, rows), F32),
            pltpu.VMEM((4, 1, rows), F32),
            pltpu.VMEM((4, 1, rows), F32),
            pltpu.VMEM((4, rows, inner), BF16),
            pltpu.VMEM((4, rows, inner), BF16),
            pltpu.VMEM((2, rows, inner), BF16),
            pltpu.VMEM((2, rows, inner), BF16),
            pltpu.VMEM((rows, inner), BF16),
            pltpu.VMEM((rows, inner), BF16),
            pltpu.VMEM((rows, inner), BF16),
            pltpu.VMEM((rows, inner), BF16),
            pltpu.VMEM((rows, inner), BF16),
            pltpu.VMEM((rows, inner), BF16),
            pltpu.VMEM((tokens, inner + 128), F32),
            pltpu.VMEM((8, share, inner + 128), F32),
            pltpu.VMEM((8, share, inner + 128), F32),
            pltpu.VMEM((8, share, inner), F32),
            pltpu.VMEM((tokens, inner), F32),
            pltpu.VMEM((tokens, inner + 128), F32),
            pltpu.VMEM((8, share, inner + 128), F32),
            pltpu.VMEM((8, share, inner + 128), F32),
            pltpu.VMEM((8, share, inner), F32),
            pltpu.VMEM((tokens, inner), F32),
            pltpu.VMEM((tokens, width), F32),
            pltpu.VMEM((tokens, width), F32),
            pltpu.VMEM((tokens, width), F32),
            dma, dma, dma, dma((8,)), dma((8,)), dma((8,)), dma, dma, dma((8,)), dma((8,)), dma((8,)),
            dma((8, 4)), dma((4,)), dma((4,)), dma((4,)),
            dma((2, 2)), dma((2,)), dma((2,)), dma((8,)), dma((8,)), dma, dma((13,)), dma((2,)),
        ],
        compiler_params=pltpu.CompilerParams(
            collective_id=0, has_side_effects=True, vmem_limit_bytes=60 * 1024 * 1024
        ),
    )(
        seq_length, gains, enc_query, enc_key, enc_value, enc_input, looked,
        cross_query_weight, attn_out_weight, cross_key_weight, cross_value_weight, cross_out_weight,
    )
    return pl.pallas_call(
        hand_kernel,
        out_shape=(
            jax.ShapeDtypeStruct((1, rows, inner), BF16),
            jax.ShapeDtypeStruct((1, rows, inner), BF16),
            jax.ShapeDtypeStruct((tokens // 2, 2, width), BF16),
        ),
        in_specs=[whole] * 3,
        out_specs=(whole, whole, whole),
    )(keys, values, decoded)


def chosen(*arrays):
    rows, inner = arrays[1].shape
    fits = lax.axis_size("ctx") == 8 and lax.axis_size("tp") == 2 and (rows, inner) == (128, 4 * HD)
    return (local_fused if fits else local)(*arrays)


def solution(mesh):
    placed = (
        P(("groups", "ctx"), None),
        P(("groups", "ctx"), "tp"),
        P(("groups", "ctx"), "tp"),
        P(("groups", "ctx"), "tp"),
        P("groups"),
        P("tp", None),
        P(),
        P("ctx", "tp"),
        P("ctx", "tp"),
        P("tp", "ctx"),
        P("groups", None),
        P("ctx"),
        P("ctx", "tp"),
        P("tp", "ctx"),
    )
    return jax.shard_map(
        chosen,
        mesh=mesh,
        in_specs=placed,
        out_specs=(
            P(("groups", "ctx"), None, "tp"),
            P(("groups", "ctx"), None, "tp"),
            P("groups", None, "ctx"),
        ),
        check_vma=False,
    )
```

time: 101 us -> 90.4 us (0.90)
  Pallas kernels: 95.1 us -> 86.8 us
  local copies, waits for them, and re-layouts: 3.94 us -> 1.4 us
    pallas_call x1, Pallas kernels: 90.3 us -> 82 us  [local_fused(): pl.pallas_call(fused_kernel, out_shape=(jax.ShapeDtypeStruct((rows, inner...]
where the time goes in v1:
time: 90.4 us; the launch traced here: 90.1 us
  Pallas kernels  86.8 us (96%)
  local copies, waits for them, and re-layouts  1.4 us (2%)
  between operations  1.3 us (1%)
    pallas_call x1, Pallas kernels, local_fused(): pl.pallas_call(fused_kernel, out_shape=(jax.ShapeDtypeStruct((rows, inner...  82 us
    pallas_call x1, Pallas kernels, local_fused(): pl.pallas_call(pick_kernel, out_shape=jax.ShapeDtypeStruct((tokens, width...  3.03 us

profile of v1, /device:TPU:0, one launch (start us, length us, event | category | flops | bytes accessed | tf_op | source)
XLA Modules:
  0.0 90.1 jit_solution(9276147838185059254)
XLA Ops:
  1.3 0.7 reshape.10
  2.0 0.7 broadcast_in_dim.2
  2.7 0.6 maximum_convert_fusion.gains
  3.3 3.0 %shard_map.157.looked_hbm = bf16[32,512]{1,0:T(8,128)(2,1)} custom-call(s32[2,16]{1,0:T(2,128)} %bitcast.1, bf16[16064,512]{1,0:T(8,128)(2,1)} %table_ref.1), custom_call_target="tpu_custom_call" | custom-call | tf_op jit(solution)/shard_map/pallas_call | solution.py:548
  6.3 82.0 %shard_map.158 = (bf16[128,512]{1,0:T(8,128)(2,1)}, bf16[128,512]{1,0:T(8,128)(2,1)}, f32[32,512]{1,0:T(8,128)}) custom-call(s32[1]{0:T(128)S(6)} %copy.17.length, f32[16,512]{1,0:T(8,128)} %maximum_convert_fusion.gains, bf16[128,512]{1,0:T(8,128)(2,1)} %q.1, bf16[128,512]{1,0:T(8,128)(2,1)} %k.1, bf16[128,512]{1,0:T(8,128)(2,1)} %v.1, ...), custom_call_target="tpu_custom_call" | custom-call | tf_op jit(solution)/shard_map/pallas_call | solution.py:559
  88.4 1.7 %shard_map.159 = (bf16[1,128,512]{2,1,0:T(8,128)(2,1)}, bf16[1,128,512]{2,1,0:T(8,128)(2,1)}, bf16[16,2,512]{2,1,0:T(2,128)(2,1)}) custom-call(bf16[128,512]{1,0:T(8,128)(2,1)} %get-tuple-element.6.keys_ref, bf16[128,512]{1,0:T(8,128)(2,1)} %get-tuple-element.7.values_ref, f32[32,512]{1,0:T(8,128)} %get-tuple-element.8.decoded_ref), custom_call_target="tpu_custom_call" | custom-call | tf_op jit(solution)/shard_map/pallas_call | solution.py:624

commit v2 on v1

--- a/solution.py
+++ b/solution.py
@@ -207,15 +207,20 @@
     q_own, q_turned, ein_own, ein_turned, looked, looked_far, wq_own, wout_own,
     kg, vg, qg, eg, wo_all, wk_all, wv_all, ctx_all, gained, square_own, square_far, square_sum, square_in,
     part_k, part_v, pair_k, pair_v, near_k, near_v, far_k, far_v, keys_own, values_own,
-    raw_own, raw_out, raw_in, query_in, query_all, mix_own, mix_out, mix_in, attn_in, attn_all, proj_out, proj_in, hidden_ref,
-    send, r_look, r_wo, r_q, r_k, r_v, r_wk, r_wv, r_raw, r_query, r_ein, r_ctx, r_gained, r_square_far, r_square,
-    r_pair, r_near, r_far, r_mix, r_attn, r_proj, fetched, stored,
+    raw_own, raw_out, raw_in, query_in, query_all, mix_own, mix_in, stat_own, stat_in, proj_out, proj_in, hidden_ref,
+    send, r_look, r_wo, r_q, r_k, r_v, r_wk, r_wv, t_wk, t_wv, r_raw, r_query, r_ein, r_ctx, r_gained, r_square_far, r_square,
+    r_pair, r_near, r_far, r_mix, r_stat, r_proj, fetched, stored,
 ):
+    g = lax.axis_index("groups")
     c = lax.axis_index("ctx")
     t = lax.axis_index("tp")
     z, y = lax.div(c, 2), lax.rem(c, 2)
     mate, other = c + 1 - 2 * y, 1 - t
     line = [lax.rem(z + d, 4) for d in (2, 1, 3)]
+    near_z = z + 1 - 2 * lax.rem(z, 2)
+    across = 2 - 2 * lax.div(z, 2)
+    across_middle = 2 - lax.div(z, 2)
+    in_middle = (z == 1) | (z == 2)
     peers = [lax.rem(c + d, 8) for d in range(1, 8)]
     rows = q.shape[0]
     inner = q.shape[1]
@@ -237,6 +242,14 @@
         copy.start()
         pending.append(copy)
 
+    def put_twin(source, target, arrival):
+        copy = pltpu.make_async_remote_copy(
+            src_ref=source, dst_ref=target, send_sem=send, recv_sem=arrival,
+            device_id={"groups": 1 - g, "ctx": c, "tp": t}, device_id_type=MESH,
+        )
+        copy.start()
+        pending.append(copy)
+
     def got(target, arrival):
         remote(target, target, arrival, mate, t).wait_recv()
 
@@ -252,6 +265,7 @@
     for peer in peers:
         pl.semaphore_signal(barrier, inc=1, device_id={"ctx": peer, "tp": t}, device_id_type=MESH)
     pl.semaphore_signal(barrier, inc=1, device_id={"ctx": c, "tp": other}, device_id_type=MESH)
+    pl.semaphore_signal(barrier, inc=1, device_id={"groups": 1 - g, "ctx": c, "tp": t}, device_id_type=MESH)
 
     q_fetch = fetch(q, q_own, fetched.at[0])
     k_fetch = fetch(k.at[:, cols(z, HD)], kg.at[c], fetched.at[1])
@@ -267,7 +281,7 @@
         fetch(wv, wv_all.at[y], fetched.at[11]),
     ]
     wout_fetch = fetch(wout, wout_own, fetched.at[12])
-    pl.semaphore_wait(barrier, len(peers) + 1)
+    pl.semaphore_wait(barrier, len(peers) + 2)
 
     for far in line:
         to = far * 2 + y
@@ -291,6 +305,28 @@
         )
     qg[c] = q_turned[y, :, cols(z, HD)]
     put(wo.at[:, cols(z * 2 + other, width)], wo_all.at[cols(t, inner)], r_wo, c, other)
+    piece = width // 4
+
+    def weight_rows(index):
+        return pl.ds(pl.multiple_of(index * piece, piece), piece)
+
+    def send_weight(weight, whole, arrivals):
+        for part in range(2):
+            where = weight_rows(g * 2 + part)
+            put(weight.at[where], whole.at[y, where], arrivals.at[part], mate, t)
+
+    def relay_weight(whole, arrivals, twins):
+        for part in range(2):
+            where = weight_rows(g * 2 + part)
+            here = whole.at[1 - y, where]
+            got(here, arrivals.at[part])
+            put_twin(here, here, twins.at[part])
+
+    def whole_weight(whole, twins):
+        for part in range(2):
+            got(whole.at[1 - y, weight_rows((1 - g) * 2 + part)], twins.at[part])
+
+    send_weight(wk, wk_all, r_wk)
 
     for far in range(4):
         ein_fetches[far].wait()
@@ -307,8 +343,8 @@
     for peer in peers:
         put(ein_turned.at[lax.div(peer, 2), lax.rem(peer, 2)], eg.at[c], r_ein.at[c], peer, t)
     eg[c] = ein_turned[z, y]
-    put(wk, wk_all.at[y], r_wk, mate, t)
-    put(wv, wv_all.at[y], r_wv, mate, t)
+    send_weight(wv, wv_all, r_wv)
+    relay_weight(wk_all, r_wk, t_wk)
 
     tokens = looked.shape[0]
     looked_fetch.wait()
@@ -343,8 +379,8 @@
         mixed = jnp.dot(probs.astype(BF16), every_value, preferred_element_type=F32)
         ctx_all[chunk, :, cols(t * 4 + z, HD)] = (mixed / total).astype(BF16)
         here, arrival = block_at(t, z, chunk)
-        for far in line:
-            put(here, here, arrival, far * 2 + y, t)
+        put(here, here, arrival, across_middle * 2 + y, t)
+        put(here, here, arrival, near_z * 2 + y, t)
         put(here, here, arrival, c, other)
 
     got(looked_far, r_look)
@@ -360,6 +396,7 @@
     for peer in peers:
         put(raw_out.at[peer], raw_in.at[c], r_raw.at[c], peer, t)
     raw_in[c] = raw_out[c]
+    relay_weight(wv_all, r_wv, t_wv)
 
     for copy in late:
         copy.wait()
@@ -370,9 +407,15 @@
     gain = jnp.sum(jnp.where(picked_gain, gains[8:16], 0.0), axis=0, keepdims=True)
 
     def relay(chunk):
-        for far in line:
+        for far in (near_z, across, across + 1):
             here, arrival = block_at(t, far, chunk)
             got(here, arrival)
+            if far is not near_z:
+
+                @pl.when(in_middle)
+                def _():
+                    remote(here, here, arrival, near_z * 2 + y, t).start()
+
             put(here, here, arrival, c, other)
 
     def project(chunk):
@@ -386,7 +429,7 @@
         put(gained.at[chunk, t], gained.at[chunk, t], r_gained.at[chunk], c, other)
         put(square_own.at[chunk], square_far.at[chunk], r_square_far.at[chunk], c, other)
 
-    ways = ((part_k, pair_k, near_k, far_k, wk_all, r_wk), (part_v, pair_v, near_v, far_v, wv_all, r_wv))
+    ways = ((part_k, pair_k, near_k, far_k, wk_all, t_wk), (part_v, pair_v, near_v, far_v, wv_all, t_wv))
 
     def start_only(source, target, arrival, to_z):
         remote(source, target, arrival, to_z * 2 + y, t).start()
@@ -396,7 +439,7 @@
         end = 0 if chunk >= 2 else 3
         for way, (part, pair, near, far, weight, arrival) in enumerate(ways):
             if first:
-                got(weight.at[1 - y], arrival)
+                whole_weight(weight, arrival)
             total = jnp.dot(gained[chunk, 0], weight[0], preferred_element_type=F32)
             total = total + jnp.dot(gained[chunk, 1], weight[1], preferred_element_type=F32)
             part[chunk] = total.astype(BF16)
@@ -475,49 +518,55 @@
         stores.append(fetch(own, out, stored.at[way]))
 
     own_valid = lax.broadcasted_iota(jnp.int32, (1, rows), 1) * 8 + c < limit
-    lanes = lax.broadcasted_iota(jnp.int32, (tokens, 128), 1)
-    stats = jnp.zeros((tokens, 128), F32)
-    for head in range(heads):
-        part = slice(head * HD, (head + 1) * HD)
-        scores = lax.dot_general(
-            query_all[:, part].astype(BF16), keys_own[:, part], (((1,), (1,)), ((), ())),
+    scores = jnp.concatenate(
+        [
+            lax.dot_general(
+                query_all[:, h * HD : (h + 1) * HD].astype(BF16), keys_own[:, h * HD : (h + 1) * HD],
+                (((1,), (1,)), ((), ())), preferred_element_type=F32,
+            )
+            for h in range(heads)
+        ],
+        axis=0,
+    )
+    scores = jnp.where(own_valid, scores, FLOOR)
+    top = jnp.max(scores, axis=-1, keepdims=True)
+    probs = jnp.where(own_valid, jnp.exp(scores - top), 0.0)
+    total = jnp.sum(probs, axis=-1, keepdims=True)
+    stat_own[0:1] = jnp.sum(jnp.where(place == spot, top, 0.0), axis=0, keepdims=True)
+    stat_own[1:2] = jnp.sum(jnp.where(place == spot, total, 0.0), axis=0, keepdims=True)
+    for h in range(heads):
+        mix_own[h * tokens : (h + 1) * tokens] = jnp.dot(
+            probs[h * tokens : (h + 1) * tokens].astype(BF16), values_own[:, h * HD : (h + 1) * HD],
             preferred_element_type=F32,
+        ).astype(BF16)
+    for peer in peers:
+        put(stat_own, stat_in.at[c], r_stat.at[c], peer, t)
+        put(mix_own, mix_in.at[c], r_mix.at[c], peer, t)
+    stat_in[c] = stat_own[...]
+    mix_in[c] = mix_own[...]
+    wout_fetch.wait()
+    for peer in peers:
+        got(stat_in.at[peer], r_stat.at[peer])
+    top = stat_in[0][0:1]
+    for j in range(1, 8):
+        top = jnp.maximum(top, stat_in[j][0:1])
+    factors = [jnp.exp(stat_in[j][0:1] - top) for j in range(8)]
+    total = factors[0] * stat_in[0][1:2]
+    for j in range(1, 8):
+        total = total + factors[j] * stat_in[j][1:2]
+    for peer in peers:
+        got(mix_in.at[peer], r_mix.at[peer])
+    mixed = jnp.zeros((rows, HD), F32)
+    for j in range(8):
+        column = jnp.sum(jnp.where(place == spot, factors[j] / total, 0.0), axis=-1, keepdims=True)
+        mixed = mixed + mix_in[j].astype(F32) * column
+    attn = mixed.astype(BF16)
+    proj = jnp.zeros(proj_out.shape, F32)
+    for h in range(heads):
+        proj = proj + jnp.dot(
+            attn[h * tokens : (h + 1) * tokens], wout_own[h * HD : (h + 1) * HD], preferred_element_type=F32
         )
-        scores = jnp.where(own_valid, scores, FLOOR)
-        top = jnp.max(scores, axis=-1, keepdims=True)
-        probs = jnp.where(own_valid, jnp.exp(scores - top), 0.0)
-        stats = jnp.where(lanes == head, top, stats)
-        stats = jnp.where(lanes == heads + head, jnp.sum(probs, axis=-1, keepdims=True), stats)
-        mix_own[:, part] = jnp.dot(probs.astype(BF16), values_own[:, part], preferred_element_type=F32)
-    mix_own[:, inner:] = stats
-    for j in range(8):
-        mix_out[j] = mix_own[j * share : (j + 1) * share, :]
-    for peer in peers:
-        put(mix_out.at[peer], mix_in.at[c], r_mix.at[c], peer, t)
-    mix_in[c] = mix_out[c]
-    for peer in peers:
-        got(mix_in.at[peer], r_mix.at[peer])
-    for head in range(heads):
-        part = slice(head * HD, (head + 1) * HD)
-        tops = [mix_in[j][:, inner + head : inner + head + 1] for j in range(8)]
-        top = tops[0]
-        for j in range(1, 8):
-            top = jnp.maximum(top, tops[j])
-        total = jnp.zeros_like(top)
-        mixed = jnp.zeros((share, HD), F32)
-        for j in range(8):
-            weight = jnp.exp(tops[j] - top)
-            total = total + mix_in[j][:, inner + heads + head : inner + heads + head + 1] * weight
-            mixed = mixed + mix_in[j][:, part] * weight
-        attn_in[c, :, part] = (mixed / total).astype(BF16).astype(F32)
-    for peer in peers:
-        put(attn_in.at[c], attn_in.at[c], r_attn.at[c], peer, t)
-    for peer in peers:
-        got(attn_in.at[peer], r_attn.at[peer])
-    for j in range(8):
-        attn_all[j * share : (j + 1) * share, :] = attn_in[j]
-    wout_fetch.wait()
-    proj_out[...] = jnp.dot(attn_all[...].astype(BF16), wout_own[...], preferred_element_type=F32)
+    proj_out[...] = proj
     put(proj_out, proj_in, r_proj, c, other)
     got(proj_in, r_proj)
     decoded_out[...] = proj_out[...] + proj_in[...] + hidden_ref[...]
@@ -527,6 +576,11 @@
         copy.wait_send()
     for i in range(6):
         remote(near_k, near_k, r_near.at[0], mate, t).wait_send()
+
+    @pl.when(in_middle)
+    def _():
+        for i in range(8):
+            remote(ctx_all.at[0, :, cols(z, HD)], ctx_all.at[0, :, cols(z, HD)], r_near.at[0], mate, t).wait_send()
 
 
 def local_fused(
@@ -602,15 +656,14 @@
             pltpu.VMEM((8, share, inner + 128), F32),
             pltpu.VMEM((8, share, inner), F32),
             pltpu.VMEM((tokens, inner), F32),
-            pltpu.VMEM((tokens, inner + 128), F32),
-            pltpu.VMEM((8, share, inner + 128), F32),
-            pltpu.VMEM((8, share, inner + 128), F32),
-            pltpu.VMEM((8, share, inner), F32),
-            pltpu.VMEM((tokens, inner), F32),
+            pltpu.VMEM((rows, HD), BF16),
+            pltpu.VMEM((8, rows, HD), BF16),
+            pltpu.VMEM((2, rows), F32),
+            pltpu.VMEM((8, 2, rows), F32),
             pltpu.VMEM((tokens, width), F32),
             pltpu.VMEM((tokens, width), F32),
             pltpu.VMEM((tokens, width), F32),
-            dma, dma, dma, dma((8,)), dma((8,)), dma((8,)), dma, dma, dma((8,)), dma((8,)), dma((8,)),
+            dma, dma, dma, dma((8,)), dma((8,)), dma((8,)), dma((2,)), dma((2,)), dma((2,)), dma((2,)), dma((8,)), dma((8,)), dma((8,)),
             dma((8, 4)), dma((4,)), dma((4,)), dma((4,)),
             dma((2, 2)), dma((2,)), dma((2,)), dma((8,)), dma((8,)), dma, dma((13,)), dma((2,)),
         ],

time: 90.4 us -> 88.8 us (0.982)
  Pallas kernels: 86.8 us -> 85.3 us
    pallas_call x1, Pallas kernels: 82 us -> 80.5 us  [local_fused(): pl.pallas_call(fused_kernel, out_shape=(jax.ShapeDtypeStruct((rows, inner...]
where the time goes in v2:
time: 88.8 us; the launch traced here: 88.6 us
  Pallas kernels  85.3 us (96%)
  local copies, waits for them, and re-layouts  1.4 us (2%)
  between operations  1.3 us (1%)
    pallas_call x1, Pallas kernels, local_fused(): pl.pallas_call(fused_kernel, out_shape=(jax.ShapeDtypeStruct((rows, inner...  80.5 us
    pallas_call x1, Pallas kernels, local_fused(): pl.pallas_call(pick_kernel, out_shape=jax.ShapeDtypeStruct((tokens, width...  3.13 us

profile of v2, /device:TPU:0, one launch (start us, length us, event | category | flops | bytes accessed | tf_op | source)
XLA Modules:
  0.0 88.6 jit_solution(16880070009713256064)
XLA Ops:
  1.3 0.7 reshape.10
  2.0 0.7 broadcast_in_dim.2
  2.7 0.6 maximum_convert_fusion.gains
  3.3 3.1 %shard_map.157.looked_hbm = bf16[32,512]{1,0:T(8,128)(2,1)} custom-call(s32[2,16]{1,0:T(2,128)} %bitcast.1, bf16[16064,512]{1,0:T(8,128)(2,1)} %table_ref.1), custom_call_target="tpu_custom_call" | custom-call | tf_op jit(solution)/shard_map/pallas_call | solution.py:602
  6.4 80.5 %shard_map.158 = (bf16[128,512]{1,0:T(8,128)(2,1)}, bf16[128,512]{1,0:T(8,128)(2,1)}, f32[32,512]{1,0:T(8,128)}) custom-call(s32[1]{0:T(128)S(6)} %copy.17.length, f32[16,512]{1,0:T(8,128)} %maximum_convert_fusion.gains, bf16[128,512]{1,0:T(8,128)(2,1)} %q.1, bf16[128,512]{1,0:T(8,128)(2,1)} %k.1, bf16[128,512]{1,0:T(8,128)(2,1)} %v.1, ...), custom_call_target="tpu_custom_call" | custom-call | tf_op jit(solution)/shard_map/pallas_call | solution.py:613
  86.9 1.7 %shard_map.159 = (bf16[1,128,512]{2,1,0:T(8,128)(2,1)}, bf16[1,128,512]{2,1,0:T(8,128)(2,1)}, bf16[16,2,512]{2,1,0:T(2,128)(2,1)}) custom-call(bf16[128,512]{1,0:T(8,128)(2,1)} %get-tuple-element.6.keys_ref, bf16[128,512]{1,0:T(8,128)(2,1)} %get-tuple-element.7.values_ref, f32[32,512]{1,0:T(8,128)} %get-tuple-element.8.decoded_ref), custom_call_target="tpu_custom_call" | custom-call | tf_op jit(solution)/shard_map/pallas_call | solution.py:677

commit v3 on v2

--- a/solution.py
+++ b/solution.py
@@ -172,28 +172,6 @@
 ORDER = (3, 0, 2, 1)
 
 
-def pick_kernel(ids_ref, table_ref, out_ref, held, rows, sems):
-    count = out_ref.shape[0]
-    vocab_local = table_ref.shape[0]
-    base = lax.axis_index("tp") * vocab_local
-    copies = []
-    for j in range(count):
-        own = jnp.clip(ids_ref[j % 2, j // 2] - base, 0, vocab_local - 1)
-        start = pl.multiple_of(lax.div(own, 16) * 16, 16)
-        copy = pltpu.make_async_copy(table_ref.at[pl.ds(start, 16)], held.at[j], sems.at[j])
-        copy.start()
-        copies.append(copy)
-    spots = lax.broadcasted_iota(jnp.int32, held.shape[1:], 0)
-    for j in range(count):
-        copies[j].wait()
-        own = ids_ref[j % 2, j // 2] - base
-        inside = (own >= 0) & (own < vocab_local)
-        spot = jnp.where(inside, lax.rem(jnp.clip(own, 0, vocab_local - 1), 16), -1)
-        block = held[j].astype(F32)
-        rows[pl.ds(j, 1)] = jnp.sum(jnp.where(spots == spot, block, 0.0), axis=0, keepdims=True)
-    out_ref[...] = rows[...].astype(BF16)
-
-
 def hand_kernel(keys_ref, values_ref, decoded_ref, keys_out, values_out, decoded_out):
     keys_out[0] = keys_ref[...]
     values_out[0] = values_ref[...]
@@ -202,9 +180,9 @@
 
 
 def fused_kernel(
-    length, gains, q, k, v, ein, looked_hbm, wq, wo, wk, wv, wout,
+    ids, length, dec_gain, enc_gain, q, k, v, ein, table, wq, wo, wk, wv, wout,
     keys_out, values_out, decoded_out,
-    q_own, q_turned, ein_own, ein_turned, looked, looked_far, wq_own, wout_own,
+    q_own, q_turned, ein_own, ein_turned, table_own, rows_own, looked, looked_far, wq_own, wout_own,
     kg, vg, qg, eg, wo_all, wk_all, wv_all, ctx_all, gained, square_own, square_far, square_sum, square_in,
     part_k, part_v, pair_k, pair_v, near_k, near_v, far_k, far_v, keys_own, values_own,
     raw_own, raw_out, raw_in, query_in, query_all, mix_own, mix_in, stat_own, stat_in, proj_out, proj_in, hidden_ref,
@@ -273,7 +251,7 @@
     ein_fetches = [
         fetch(ein.at[:, cols(far * 2 + t, width)], ein_own.at[far], fetched.at[3 + far]) for far in range(4)
     ]
-    looked_fetch = fetch(looked_hbm, looked, fetched.at[7])
+    table_fetch = fetch(table, table_own, fetched.at[7])
     wq_fetch = fetch(wq, wq_own, fetched.at[8])
     late = [
         fetch(wo.at[:, cols(own_block, width)], wo_all.at[cols(t, inner)], fetched.at[9]),
@@ -328,27 +306,49 @@
 
     send_weight(wk, wk_all, r_wk)
 
+    tokens = looked.shape[0]
     for far in range(4):
         ein_fetches[far].wait()
         turned = jnp.dot(turn, ein_own[far], preferred_element_type=F32).astype(BF16)
         for s in range(2):
             ein_turned[far, s] = turned[s * half : (s + 1) * half]
 
+    for peer in peers:
+        put(ein_turned.at[lax.div(peer, 2), lax.rem(peer, 2)], eg.at[c], r_ein.at[c], peer, t)
+    eg[c] = ein_turned[z, y]
     for far in line:
         source = far * 2 + y
         got(kg.at[source], r_k.at[source])
         put(kg.at[source], kg.at[source], r_k.at[source], mate, t)
         got(vg.at[source], r_v.at[source])
         put(vg.at[source], vg.at[source], r_v.at[source], mate, t)
-    for peer in peers:
-        put(ein_turned.at[lax.div(peer, 2), lax.rem(peer, 2)], eg.at[c], r_ein.at[c], peer, t)
-    eg[c] = ein_turned[z, y]
     send_weight(wv, wv_all, r_wv)
     relay_weight(wk_all, r_wk, t_wk)
 
-    tokens = looked.shape[0]
-    looked_fetch.wait()
+    table_fetch.wait()
+    first = t * table.shape[0] * 16
+    spots = lax.broadcasted_iota(jnp.int32, (16, width), 0)
+    for j in range(tokens):
+        own = ids[j % 2, j // 2] - first
+        near = jnp.clip(own, 0, table.shape[0] * 16 - 1)
+        block = table_own[lax.div(near, 16)].astype(F32)
+        picked = spots + lax.div(near, 16) * 16 == own
+        rows_own[j : j + 1] = jnp.sum(jnp.where(picked, block, 0.0), axis=0, keepdims=True)
+    looked[...] = rows_own[...].astype(BF16)
     put(looked, looked_far, r_look, c, other)
+    got(looked_far, r_look)
+    wq_fetch.wait()
+    hidden = looked[...].astype(F32) + looked_far[...].astype(F32)
+    hidden_ref[...] = hidden
+    scaled = (hidden * dec_gain[...].astype(F32).reshape(1, width)).astype(BF16)
+    raw_own[:, :inner] = jnp.dot(scaled, wq_own[...], preferred_element_type=F32)
+    raw_own[:, inner:] = jnp.broadcast_to(jnp.sum(hidden * hidden, axis=-1, keepdims=True), (tokens, 128))
+    share = tokens // 8
+    for j in range(8):
+        raw_out[j] = raw_own[j * share : (j + 1) * share, :]
+    for peer in peers:
+        put(raw_out.at[peer], raw_in.at[c], r_raw.at[c], peer, t)
+    raw_in[c] = raw_out[c]
 
     k_fetch.wait()
     v_fetch.wait()
@@ -383,19 +383,6 @@
         put(here, here, arrival, near_z * 2 + y, t)
         put(here, here, arrival, c, other)
 
-    got(looked_far, r_look)
-    wq_fetch.wait()
-    hidden = looked[...].astype(F32) + looked_far[...].astype(F32)
-    hidden_ref[...] = hidden
-    scaled = (hidden * gains[0:1]).astype(BF16)
-    raw_own[:, :inner] = jnp.dot(scaled, wq_own[...], preferred_element_type=F32)
-    raw_own[:, inner:] = jnp.broadcast_to(jnp.sum(hidden * hidden, axis=-1, keepdims=True), (tokens, 128))
-    share = tokens // 8
-    for j in range(8):
-        raw_out[j] = raw_own[j * share : (j + 1) * share, :]
-    for peer in peers:
-        put(raw_out.at[peer], raw_in.at[c], r_raw.at[c], peer, t)
-    raw_in[c] = raw_out[c]
     relay_weight(wv_all, r_wv, t_wv)
 
     for copy in late:
@@ -403,8 +390,7 @@
     got(wo_all.at[cols(other, inner)], r_wo)
     for peer in peers:
         got(eg.at[peer], r_ein.at[peer])
-    picked_gain = lax.broadcasted_iota(jnp.int32, (8, width), 0) == own_block
-    gain = jnp.sum(jnp.where(picked_gain, gains[8:16], 0.0), axis=0, keepdims=True)
+    gain = enc_gain[cols(own_block, width)].astype(F32).reshape(1, width)
 
     def relay(chunk):
         for far in (near_z, across, across + 1):
@@ -450,9 +436,18 @@
                     part.at[chunk], pair.at[chunk % 2], r_pair.at[way, chunk % 2], 1 if end == 0 else 2
                 )
 
-            @pl.when(z == (chunk + 1 if chunk % 2 == 0 else chunk - 1))
+            if chunk in (0, 3):
+
+                @pl.when(z == (1 if chunk == 0 else 2))
+                def _():
+                    start_only(part.at[chunk], near, r_near.at[way], chunk)
+
+    def last_near():
+        for way, (part, pair, near, far, weight, arrival) in enumerate(ways):
+
+            @pl.when((z == 0) | (z == 3))
             def _():
-                start_only(part.at[chunk], near, r_near.at[way], chunk)
+                start_only(part.at[near_z], near, r_near.at[way], near_z)
 
     def join(chunk):
         middle = 1 if chunk >= 2 else 2
@@ -469,14 +464,15 @@
     relay(ORDER[1])
     project(ORDER[0])
     relay(ORDER[2])
+    spread_out(ORDER[0], True)
     project(ORDER[1])
-    spread_out(ORDER[0], True)
     relay(ORDER[3])
+    spread_out(ORDER[1], False)
     project(ORDER[2])
-    spread_out(ORDER[1], False)
+    spread_out(ORDER[2], False)
     project(ORDER[3])
-    spread_out(ORDER[2], False)
     spread_out(ORDER[3], False)
+    last_near()
     for chunk in range(4):
         got(square_far.at[chunk], r_square_far.at[chunk])
         square_sum[chunk] = square_own[chunk] + square_far[chunk]
@@ -509,14 +505,16 @@
         query_all[j * share : (j + 1) * share, :] = query_in[j]
 
     stores = []
-    for way, (own, out) in enumerate(((keys_own, keys_out), (values_own, values_out))):
+
+    def settle(way, own, out):
         part, pair, near, far, weight, arrival = ways[way]
+        got(far, r_far.at[way])
         got(near, r_near.at[way])
-        got(far, r_far.at[way])
         total = part[z].astype(F32) + near[...].astype(F32) + far[...].astype(F32)
         own[...] = (total * scale).astype(BF16)
         stores.append(fetch(own, out, stored.at[way]))
 
+    settle(0, keys_own, keys_out)
     own_valid = lax.broadcasted_iota(jnp.int32, (1, rows), 1) * 8 + c < limit
     scores = jnp.concatenate(
         [
@@ -534,13 +532,15 @@
     total = jnp.sum(probs, axis=-1, keepdims=True)
     stat_own[0:1] = jnp.sum(jnp.where(place == spot, top, 0.0), axis=0, keepdims=True)
     stat_own[1:2] = jnp.sum(jnp.where(place == spot, total, 0.0), axis=0, keepdims=True)
+    for peer in peers:
+        put(stat_own, stat_in.at[c], r_stat.at[c], peer, t)
+    settle(1, values_own, values_out)
     for h in range(heads):
         mix_own[h * tokens : (h + 1) * tokens] = jnp.dot(
             probs[h * tokens : (h + 1) * tokens].astype(BF16), values_own[:, h * HD : (h + 1) * HD],
             preferred_element_type=F32,
         ).astype(BF16)
     for peer in peers:
-        put(stat_own, stat_in.at[c], r_stat.at[c], peer, t)
         put(mix_own, mix_in.at[c], r_mix.at[c], peer, t)
     stat_in[c] = stat_own[...]
     mix_in[c] = mix_own[...]
@@ -593,23 +593,9 @@
     whole = pl.BlockSpec(memory_space=pltpu.VMEM)
     scalars = pl.BlockSpec(memory_space=pltpu.SMEM)
     anywhere = pl.BlockSpec(memory_space=pl.ANY)
-    gains = jnp.concatenate(
-        [jnp.broadcast_to(dec_gain[None], (8, width)), enc_gain.reshape(8, width)], axis=0
-    ).astype(F32)
     dma = pltpu.SemaphoreType.DMA
     share = tokens // 8
     half = rows // 2
-    looked = pl.pallas_call(
-        pick_kernel,
-        out_shape=jax.ShapeDtypeStruct((tokens, width), BF16),
-        in_specs=[scalars, anywhere],
-        out_specs=whole,
-        scratch_shapes=[
-            pltpu.VMEM((tokens, 16, width), BF16),
-            pltpu.VMEM((tokens, width), F32),
-            pltpu.SemaphoreType.DMA((tokens,)),
-        ],
-    )(dec_ids.T, embed_table)
     keys, values, decoded = pl.pallas_call(
         fused_kernel,
         out_shape=(
@@ -617,13 +603,15 @@
             jax.ShapeDtypeStruct((rows, inner), BF16),
             jax.ShapeDtypeStruct((tokens, width), F32),
         ),
-        in_specs=[scalars, whole] + [anywhere] * 10,
+        in_specs=[scalars, scalars, whole, whole] + [anywhere] * 10,
         out_specs=(anywhere, anywhere, whole),
         scratch_shapes=[
             pltpu.VMEM((rows, inner), BF16),
             pltpu.VMEM((2, half, inner), BF16),
             pltpu.VMEM((4, rows, width), BF16),
             pltpu.VMEM((4, 2, half, width), BF16),
+            pltpu.VMEM((embed_table.shape[0] // 16, 16, width), BF16),
+            pltpu.VMEM((tokens, width), F32),
             pltpu.VMEM((tokens, width), BF16),
             pltpu.VMEM((tokens, width), BF16),
             pltpu.VMEM((width, inner), BF16),
@@ -671,7 +659,8 @@
             collective_id=0, has_side_effects=True, vmem_limit_bytes=60 * 1024 * 1024
         ),
     )(
-        seq_length, gains, enc_query, enc_key, enc_value, enc_input, looked,
+        dec_ids.T, seq_length, dec_gain, enc_gain, enc_query, enc_key, enc_value, enc_input,
+        embed_table.reshape(embed_table.shape[0] // 16, 16, width),
         cross_query_weight, attn_out_weight, cross_key_weight, cross_value_weight, cross_out_weight,
     )
     return pl.pallas_call(
@@ -689,6 +678,7 @@
 def chosen(*arrays):
     rows, inner = arrays[1].shape
     fits = lax.axis_size("ctx") == 8 and lax.axis_size("tp") == 2 and (rows, inner) == (128, 4 * HD)
+    fits = fits and arrays[9].shape[0] % 16 == 0
     return (local_fused if fits else local)(*arrays)
 
 

time: 88.8 us -> 78.4 us (0.88)
  Pallas kernels: 85.3 us -> 76.9 us
  local copies, waits for them, and re-layouts: 1.4 us -> 0 us
    pallas_call x1, Pallas kernels: 80.5 us -> 75.3 us  [local_fused(): pl.pallas_call(fused_kernel, out_shape=(jax.ShapeDtypeStruct((rows, inner...]
    pallas_call x1 -> x0, Pallas kernels: 3.13 us -> none  [local_fused(): pl.pallas_call(pick_kernel, out_shape=jax.ShapeDtypeStruct((tokens, width...]
where the time goes in v3:
time: 78.4 us; the launch traced here: 78.2 us
  Pallas kernels  76.9 us (98%)
  between operations  1.29 us (2%)
    pallas_call x1, Pallas kernels, local_fused(): pl.pallas_call(fused_kernel, out_shape=(jax.ShapeDtypeStruct((rows, inner...  75.3 us
    pallas_call x1, Pallas kernels, local_fused(): pl.pallas_call(hand_kernel, out_shape=(jax.ShapeDtypeStruct((1, rows, inn...  1.68 us

profile of v3, /device:TPU:0, one launch (start us, length us, event | category | flops | bytes accessed | tf_op | source)
XLA Modules:
  0.0 78.2 jit_solution(255505749560109172)
XLA Ops:
  1.3 75.3 %shard_map.157 = (bf16[128,512]{1,0:T(8,128)(2,1)}, bf16[128,512]{1,0:T(8,128)(2,1)}, f32[32,512]{1,0:T(8,128)}) custom-call(s32[2,16]{1,0:T(2,128)} %bitcast.3, s32[1]{0:T(128)S(6)} %copy.17.length, bf16[512]{0:T(512)(128)(2,1)} %dec_gain.1, bf16[4096]{0:T(1024)(128)(2,1)} %enc_gain.1, bf16[128,512]{1,0:T(8,128)(2,1)} %q.1, bf16[128,512]{1,0:T(8,128)(2,1)} %k.1, ...), custom_call_target="tpu_custom_call" | custom-call | tf_op jit(solution)/shard_map/pallas_call | solution.py:599
  76.6 1.7 %shard_map.158 = (bf16[1,128,512]{2,1,0:T(8,128)(2,1)}, bf16[1,128,512]{2,1,0:T(8,128)(2,1)}, bf16[16,2,512]{2,1,0:T(2,128)(2,1)}) custom-call(bf16[128,512]{1,0:T(8,128)(2,1)} %get-tuple-element.6.keys_ref, bf16[128,512]{1,0:T(8,128)(2,1)} %get-tuple-element.7.values_ref, f32[32,512]{1,0:T(8,128)} %get-tuple-element.8.decoded_ref), custom_call_target="tpu_custom_call" | custom-call | tf_op jit(solution)/shard_map/pallas_call | solution.py:666

commit v4 on v3

--- a/solution.py
+++ b/solution.py
@@ -180,9 +180,9 @@
 
 
 def fused_kernel(
-    ids, length, dec_gain, enc_gain, q, k, v, ein, table, wq, wo, wk, wv, wout,
+    ids, length, dec_gain_far, enc_gain_far, q, k, v, ein, table, wq, wo, wk, wv, wout,
     keys_out, values_out, decoded_out,
-    q_own, q_turned, ein_own, ein_turned, table_own, rows_own, looked, looked_far, wq_own, wout_own,
+    dec_gain, enc_gain, q_own, q_turned, ein_own, ein_turned, table_own, rows_own, looked, looked_far, wq_own, wout_own,
     kg, vg, qg, eg, wo_all, wk_all, wv_all, ctx_all, gained, square_own, square_far, square_sum, square_in,
     part_k, part_v, pair_k, pair_v, near_k, near_v, far_k, far_v, keys_own, values_own,
     raw_own, raw_out, raw_in, query_in, query_all, mix_own, mix_in, stat_own, stat_in, proj_out, proj_in, hidden_ref,
@@ -245,6 +245,7 @@
     pl.semaphore_signal(barrier, inc=1, device_id={"ctx": c, "tp": other}, device_id_type=MESH)
     pl.semaphore_signal(barrier, inc=1, device_id={"groups": 1 - g, "ctx": c, "tp": t}, device_id_type=MESH)
 
+    gain_fetches = [fetch(dec_gain_far, dec_gain, fetched.at[13]), fetch(enc_gain_far, enc_gain, fetched.at[14])]
     q_fetch = fetch(q, q_own, fetched.at[0])
     k_fetch = fetch(k.at[:, cols(z, HD)], kg.at[c], fetched.at[1])
     v_fetch = fetch(v.at[:, cols(z, HD)], vg.at[c], fetched.at[2])
@@ -274,6 +275,8 @@
     turn = (spot == lax.rem(rest, each) * 8 + lax.div(rest, each) * 2 + side).astype(BF16)
 
     q_fetch.wait()
+    for copy in gain_fetches:
+        copy.wait()
     turned = jnp.dot(turn, q_own[...], preferred_element_type=F32).astype(BF16)
     for s in range(2):
         q_turned[s] = turned[s * half : (s + 1) * half]
@@ -313,8 +316,6 @@
         for s in range(2):
             ein_turned[far, s] = turned[s * half : (s + 1) * half]
 
-    for peer in peers:
-        put(ein_turned.at[lax.div(peer, 2), lax.rem(peer, 2)], eg.at[c], r_ein.at[c], peer, t)
     eg[c] = ein_turned[z, y]
     for far in line:
         source = far * 2 + y
@@ -323,6 +324,15 @@
         got(vg.at[source], r_v.at[source])
         put(vg.at[source], vg.at[source], r_v.at[source], mate, t)
     send_weight(wv, wv_all, r_wv)
+    def send_rows(chunk):
+        where = slice(chunk * each, (chunk + 1) * each)
+        for peer in peers:
+            put(
+                ein_turned.at[lax.div(peer, 2), lax.rem(peer, 2), where], eg.at[c, where], r_ein.at[c, chunk], peer, t
+            )
+
+    send_rows(ORDER[0])
+    send_rows(ORDER[1])
     relay_weight(wk_all, r_wk, t_wk)
 
     table_fetch.wait()
@@ -383,13 +393,12 @@
         put(here, here, arrival, near_z * 2 + y, t)
         put(here, here, arrival, c, other)
 
+    send_rows(ORDER[2])
     relay_weight(wv_all, r_wv, t_wv)
 
     for copy in late:
         copy.wait()
     got(wo_all.at[cols(other, inner)], r_wo)
-    for peer in peers:
-        got(eg.at[peer], r_ein.at[peer])
     gain = enc_gain[cols(own_block, width)].astype(F32).reshape(1, width)
 
     def relay(chunk):
@@ -407,6 +416,8 @@
     def project(chunk):
         for far in range(4):
             got(*block_at(other, far, chunk))
+        for peer in peers:
+            got(eg.at[peer, chunk * each : (chunk + 1) * each], r_ein.at[peer, chunk])
         resid = jnp.dot(ctx_all[chunk], wo_all[...], preferred_element_type=F32)
         resid = resid + eg[:, chunk * each : (chunk + 1) * each, :].reshape(rows, width).astype(F32)
         spread = jnp.where(place == spot, jnp.sum(resid * resid, axis=-1, keepdims=True), 0.0)
@@ -463,6 +474,7 @@
     relay(ORDER[0])
     relay(ORDER[1])
     project(ORDER[0])
+    send_rows(ORDER[3])
     relay(ORDER[2])
     spread_out(ORDER[0], True)
     project(ORDER[1])
@@ -603,9 +615,11 @@
             jax.ShapeDtypeStruct((rows, inner), BF16),
             jax.ShapeDtypeStruct((tokens, width), F32),
         ),
-        in_specs=[scalars, scalars, whole, whole] + [anywhere] * 10,
+        in_specs=[scalars, scalars] + [anywhere] * 12,
         out_specs=(anywhere, anywhere, whole),
         scratch_shapes=[
+            pltpu.VMEM(dec_gain.shape, BF16),
+            pltpu.VMEM(enc_gain.shape, BF16),
             pltpu.VMEM((rows, inner), BF16),
             pltpu.VMEM((2, half, inner), BF16),
             pltpu.VMEM((4, rows, width), BF16),
@@ -651,9 +665,9 @@
             pltpu.VMEM((tokens, width), F32),
             pltpu.VMEM((tokens, width), F32),
             pltpu.VMEM((tokens, width), F32),
-            dma, dma, dma, dma((8,)), dma((8,)), dma((8,)), dma((2,)), dma((2,)), dma((2,)), dma((2,)), dma((8,)), dma((8,)), dma((8,)),
+            dma, dma, dma, dma((8,)), dma((8,)), dma((8,)), dma((2,)), dma((2,)), dma((2,)), dma((2,)), dma((8,)), dma((8,)), dma((8, 4)),
             dma((8, 4)), dma((4,)), dma((4,)), dma((4,)),
-            dma((2, 2)), dma((2,)), dma((2,)), dma((8,)), dma((8,)), dma, dma((13,)), dma((2,)),
+            dma((2, 2)), dma((2,)), dma((2,)), dma((8,)), dma((8,)), dma, dma((15,)), dma((2,)),
         ],
         compiler_params=pltpu.CompilerParams(
             collective_id=0, has_side_effects=True, vmem_limit_bytes=60 * 1024 * 1024

time: 78.4 us -> 76.7 us (0.978)
  Pallas kernels: 76.9 us -> 75.2 us
    pallas_call x1, Pallas kernels: 75.3 us -> 73.5 us  [local_fused(): pl.pallas_call(fused_kernel, out_shape=(jax.ShapeDtypeStruct((rows, inner...]
where the time goes in v4:
time: 76.7 us; the launch traced here: 76.5 us
  Pallas kernels  75.2 us (98%)
  between operations  1.29 us (2%)
    pallas_call x1, Pallas kernels, local_fused(): pl.pallas_call(fused_kernel, out_shape=(jax.ShapeDtypeStruct((rows, inner...  73.5 us
    pallas_call x1, Pallas kernels, local_fused(): pl.pallas_call(hand_kernel, out_shape=(jax.ShapeDtypeStruct((1, rows, inn...  1.68 us

profile of v4, /device:TPU:0, one launch (start us, length us, event | category | flops | bytes accessed | tf_op | source)
XLA Modules:
  0.0 76.5 jit_solution(4934782570948841209)
XLA Ops:
  1.3 73.5 %shard_map.157 = (bf16[128,512]{1,0:T(8,128)(2,1)}, bf16[128,512]{1,0:T(8,128)(2,1)}, f32[32,512]{1,0:T(8,128)}) custom-call(s32[2,16]{1,0:T(2,128)} %bitcast.3, s32[1]{0:T(128)S(6)} %copy.17.length, bf16[512]{0:T(512)(128)(2,1)} %dec_gain_far.1, bf16[4096]{0:T(1024)(128)(2,1)} %enc_gain_far.1, bf16[128,512]{1,0:T(8,128)(2,1)} %q.1, bf16[128,512]{1,0:T(8,128)(2,1)} %k.1, ...), custom_call_target="tpu_custom_call" | custom-call | tf_op jit(solution)/shard_map/pallas_call | solution.py:611
  74.8 1.7 %shard_map.158 = (bf16[1,128,512]{2,1,0:T(8,128)(2,1)}, bf16[1,128,512]{2,1,0:T(8,128)(2,1)}, bf16[16,2,512]{2,1,0:T(2,128)(2,1)}) custom-call(bf16[128,512]{1,0:T(8,128)(2,1)} %get-tuple-element.6.keys_ref, bf16[128,512]{1,0:T(8,128)(2,1)} %get-tuple-element.7.values_ref, f32[32,512]{1,0:T(8,128)} %get-tuple-element.8.decoded_ref), custom_call_target="tpu_custom_call" | custom-call | tf_op jit(solution)/shard_map/pallas_call | solution.py:680

commit v5 on v4

--- a/solution.py
+++ b/solution.py
@@ -500,7 +500,7 @@
     for j in range(1, 8):
         raw = raw + raw_in[j]
     factor = lax.rsqrt(raw[:, inner : inner + 1] / D + EPSILON)
-    query_in[c] = (raw[:, :inner] * factor * HD ** (-0.5)).astype(BF16).astype(F32)
+    query_in[c] = (raw[:, :inner] * factor * HD ** (-0.5)).astype(BF16)
     for peer in peers:
         put(query_in.at[c], query_in.at[c], r_query.at[c], peer, t)
     join(ORDER[2])
@@ -514,7 +514,7 @@
     for peer in peers:
         got(query_in.at[peer], r_query.at[peer])
     for j in range(8):
-        query_all[j * share : (j + 1) * share, :] = query_in[j]
+        query_all[j * share : (j + 1) * share, :] = query_in[j].astype(F32)
 
     stores = []
 
@@ -656,7 +656,7 @@
             pltpu.VMEM((tokens, inner + 128), F32),
             pltpu.VMEM((8, share, inner + 128), F32),
             pltpu.VMEM((8, share, inner + 128), F32),
-            pltpu.VMEM((8, share, inner), F32),
+            pltpu.VMEM((8, share, inner), BF16),
             pltpu.VMEM((tokens, inner), F32),
             pltpu.VMEM((rows, HD), BF16),
             pltpu.VMEM((8, rows, HD), BF16),

time: 76.7 us -> 76.3 us (level)
  no operation moved by 1% of the time
where the time goes in v5:
time: 76.3 us; the launch traced here: 76.1 us
  Pallas kernels  74.9 us (98%)
  between operations  1.29 us (2%)
    pallas_call x1, Pallas kernels, local_fused(): pl.pallas_call(fused_kernel, out_shape=(jax.ShapeDtypeStruct((rows, inner...  73.2 us
    pallas_call x1, Pallas kernels, local_fused(): pl.pallas_call(hand_kernel, out_shape=(jax.ShapeDtypeStruct((1, rows, inn...  1.68 us

profile of v5, /device:TPU:0, one launch (start us, length us, event | category | flops | bytes accessed | tf_op | source)
XLA Modules:
  0.0 76.1 jit_solution(10125924244068677176)
XLA Ops:
  1.3 73.2 %shard_map.157 = (bf16[128,512]{1,0:T(8,128)(2,1)}, bf16[128,512]{1,0:T(8,128)(2,1)}, f32[32,512]{1,0:T(8,128)}) custom-call(s32[2,16]{1,0:T(2,128)} %bitcast.3, s32[1]{0:T(128)S(6)} %copy.17.length, bf16[512]{0:T(512)(128)(2,1)} %dec_gain_far.1, bf16[4096]{0:T(1024)(128)(2,1)} %enc_gain_far.1, bf16[128,512]{1,0:T(8,128)(2,1)} %q.1, bf16[128,512]{1,0:T(8,128)(2,1)} %k.1, ...), custom_call_target="tpu_custom_call" | custom-call | tf_op jit(solution)/shard_map/pallas_call | solution.py:611
  74.5 1.7 %shard_map.158 = (bf16[1,128,512]{2,1,0:T(8,128)(2,1)}, bf16[1,128,512]{2,1,0:T(8,128)(2,1)}, bf16[16,2,512]{2,1,0:T(2,128)(2,1)}) custom-call(bf16[128,512]{1,0:T(8,128)(2,1)} %get-tuple-element.6.keys_ref, bf16[128,512]{1,0:T(8,128)(2,1)} %get-tuple-element.7.values_ref, f32[32,512]{1,0:T(8,128)} %get-tuple-element.8.decoded_ref), custom_call_target="tpu_custom_call" | custom-call | tf_op jit(solution)/shard_map/pallas_call | solution.py:680

commit v6 on v5

--- a/solution.py
+++ b/solution.py
@@ -402,7 +402,7 @@
     gain = enc_gain[cols(own_block, width)].astype(F32).reshape(1, width)
 
     def relay(chunk):
-        for far in (near_z, across, across + 1):
+        for far in (across_middle, across * 2 + 1 - across_middle, near_z):
             here, arrival = block_at(t, far, chunk)
             got(here, arrival)
             if far is not near_z:
@@ -474,8 +474,8 @@
     relay(ORDER[0])
     relay(ORDER[1])
     project(ORDER[0])
+    relay(ORDER[2])
     send_rows(ORDER[3])
-    relay(ORDER[2])
     spread_out(ORDER[0], True)
     project(ORDER[1])
     relay(ORDER[3])
@@ -494,6 +494,7 @@
 
     join(ORDER[0])
     join(ORDER[1])
+    join(ORDER[2])
     for peer in peers:
         got(raw_in.at[peer], r_raw.at[peer])
     raw = raw_in[0]
@@ -503,7 +504,6 @@
     query_in[c] = (raw[:, :inner] * factor * HD ** (-0.5)).astype(BF16)
     for peer in peers:
         put(query_in.at[c], query_in.at[c], r_query.at[c], peer, t)
-    join(ORDER[2])
     join(ORDER[3])
 
     for far in line:

time: 76.3 us -> 76.3 us (level)
  no operation moved by 1% of the time
where the time goes in v6:
time: 76.3 us; the launch traced here: 76.1 us
  Pallas kernels  74.8 us (98%)
  between operations  1.29 us (2%)
    pallas_call x1, Pallas kernels, local_fused(): pl.pallas_call(fused_kernel, out_shape=(jax.ShapeDtypeStruct((rows, inner...  73.2 us
    pallas_call x1, Pallas kernels, local_fused(): pl.pallas_call(hand_kernel, out_shape=(jax.ShapeDtypeStruct((1, rows, inn...  1.68 us

profile of v6, /device:TPU:0, one launch (start us, length us, event | category | flops | bytes accessed | tf_op | source)
XLA Modules:
  0.0 76.1 jit_solution(11761458568658080141)
XLA Ops:
  1.3 73.2 %shard_map.157 = (bf16[128,512]{1,0:T(8,128)(2,1)}, bf16[128,512]{1,0:T(8,128)(2,1)}, f32[32,512]{1,0:T(8,128)}) custom-call(s32[2,16]{1,0:T(2,128)} %bitcast.3, s32[1]{0:T(128)S(6)} %copy.17.length, bf16[512]{0:T(512)(128)(2,1)} %dec_gain_far.1, bf16[4096]{0:T(1024)(128)(2,1)} %enc_gain_far.1, bf16[128,512]{1,0:T(8,128)(2,1)} %q.1, bf16[128,512]{1,0:T(8,128)(2,1)} %k.1, ...), custom_call_target="tpu_custom_call" | custom-call | tf_op jit(solution)/shard_map/pallas_call | solution.py:611
  74.5 1.7 %shard_map.158 = (bf16[1,128,512]{2,1,0:T(8,128)(2,1)}, bf16[1,128,512]{2,1,0:T(8,128)(2,1)}, bf16[16,2,512]{2,1,0:T(2,128)(2,1)}) custom-call(bf16[128,512]{1,0:T(8,128)(2,1)} %get-tuple-element.6.keys_ref, bf16[128,512]{1,0:T(8,128)(2,1)} %get-tuple-element.7.values_ref, f32[32,512]{1,0:T(8,128)} %get-tuple-element.8.decoded_ref), custom_call_target="tpu_custom_call" | custom-call | tf_op jit(solution)/shard_map/pallas_call | solution.py:680
